TPU v7x, 128 devices: a whole 4x4x4 slice. The times are simulated.
128 devices in a mesh: rows: 32 (over z, x, core), rep: 4 (over y).
Axes of the slice: x: 4, y: 4, z: 4, core: 2. Of those that a mesh axis runs over, the one named last changes fastest.
Arguments:
- features: bfloat16 [65536, 512], P(('rows', 'rep')), may hold values from -6 to 6
- weight: bfloat16 [512, 512], replicated, may hold values from -6 to 6
- out_bias: float32 [512], replicated, may hold values from -4 to 4
- degree: int32 [65536], P(('rows', 'rep')), may hold values from 256 to 1023
- tile_row: int32 [8192], P(('rows', 'rep')), may hold values from 0 to 15, as said below
- tile_col: int32 [8192], P(('rows', 'rep')), may hold values from 0 to 127, as said below
- tile_value: bfloat16 [8192, 128, 128], P(('rows', 'rep')), may hold values from 0 to 3, as said below
- cotangent: bfloat16 [65536, 512], P(('rows', 'rep')), may hold values from -6 to 6
Outputs:
- hidden_out: bfloat16 [65536, 512], P(('rows', 'rep'))
- grad_input: bfloat16 [65536, 512], P(('rows', 'rep'))
- grad_weight: float32 [512, 512], replicated
Inputs may be any that keep to these rules, and one draw needn't show every extreme that they name: `tile_row`: on each device the slots that hold edges come first; every later slot has an all-zero tile and both of its indices 0. Every node block's diagonal block is among its device's slots. Columns of a device's group are numbered slab by slab: tile_col = j * 4 + b names node block (j * 4 + c) * 4 + b. `tile_value`: all slots together form a symmetric adjacency: for every slot with tile V on global blocks (g, h) there is a slot on (h, g) with tile V transposed, and a diagonal block's tile is symmetric. Entries are 0 or between 0.1 and 3.
All inputs are finite; a program needn't handle non-finite values.
Results may differ from a plain program's by a relative error of at most 0.0061.
Values may be sent and summed in bfloat16 or wider, within the bound.
A program may use at most 128 MiB of HBM per device.

v0:
```python
import jax
import jax.numpy as jnp
from jax import lax
from jax.sharding import PartitionSpec as P


def aggregate_slots(panels, group_rows_all, group_cols_all, tiles_all, out_blocks):
    tile_size = tiles_all.shape[1]
    feat_width = panels.shape[1]
    panel_blocks = panels.reshape(-1, tile_size, feat_width)
    group_count = tiles_all.shape[0] // 8

    def add_group(totals, bundle):
        group_rows, group_cols, group_tiles = bundle
        products = jnp.einsum(
            "sij,sjf->sif",
            group_tiles,
            panel_blocks[group_cols],
            preferred_element_type=jnp.float32,
        )
        return (totals.at[group_rows].add(products), None)

    initial = jnp.zeros((out_blocks, tile_size, feat_width), jnp.float32)
    bundles = (
        group_rows_all.reshape(group_count, 8),
        group_cols_all.reshape(group_count, 8),
        tiles_all.reshape(group_count, 8, tile_size, tile_size),
    )
    totals, _ = lax.scan(add_group, initial, bundles)
    return totals.reshape(out_blocks * tile_size, feat_width)


def shards(features, weight, out_bias, degree, tile_row, tile_col, tile_value, cotangent):
    tile_size = tile_value.shape[1]
    nodes_dev = features.shape[0]
    feat_width = features.shape[1]
    block_count = nodes_dev // tile_size
    rep_count = lax.axis_size("rep")
    row_scale = lax.rsqrt(degree.astype(jnp.float32))[:, None]
    scaled = (jnp.dot(features, weight, preferred_element_type=jnp.float32) * row_scale).astype(
        jnp.bfloat16
    )
    panels = lax.all_gather(scaled, "rows", axis=0, tiled=True)
    slab_part = aggregate_slots(panels, tile_row, tile_col, tile_value, rep_count * block_count)
    aggregate = lax.psum_scatter(slab_part, "rep", scatter_dimension=0, tiled=True) * row_scale
    pre_act = aggregate + out_bias
    hidden_out = jax.nn.silu(pre_act).astype(jnp.bfloat16)
    sigmoid_pre = jax.nn.sigmoid(pre_act)
    grad_pre = cotangent.astype(jnp.float32) * sigmoid_pre * (1.0 + pre_act * (1.0 - sigmoid_pre))
    scaled_grad = (grad_pre * row_scale).astype(jnp.bfloat16)
    slab_grads = lax.all_gather(scaled_grad, "rep", axis=0, tiled=True)
    grad_blocks = slab_grads.reshape(rep_count * block_count, tile_size, feat_width)
    products = jnp.einsum(
        "sji,sjf->sif", tile_value, grad_blocks[tile_row], preferred_element_type=jnp.float32
    )
    block_total = nodes_dev * lax.axis_size("rows") // tile_size
    target = jnp.where((tile_col >= 0) & (tile_col < block_total), tile_col, block_total)
    totals = jnp.zeros((block_total, tile_size, feat_width), jnp.float32)
    totals = totals.at[target].add(products, mode="drop")
    back_total = lax.psum_scatter(
        totals.reshape(nodes_dev * lax.axis_size("rows"), feat_width),
        "rows",
        scatter_dimension=0,
        tiled=True,
    )
    back_sum = (back_total * row_scale).astype(jnp.bfloat16)
    grad_input = lax.dot_general(
        back_sum, weight, (((1,), (1,)), ((), ())), preferred_element_type=jnp.float32
    ).astype(jnp.bfloat16)
    local_weight = lax.dot_general(
        features, back_sum, (((0,), (0,)), ((), ())), preferred_element_type=jnp.float32
    )
    grad_weight = lax.psum(local_weight, ("rows", "rep"))
    return (hidden_out, grad_input, grad_weight)


def solution(mesh):
    placed = (
        P(("rows", "rep"), None),
        P(),
        P(),
        P(("rows", "rep")),
        P(("rows", "rep")),
        P(("rows", "rep")),
        P(("rows", "rep"), None, None),
        P(("rows", "rep"), None),
    )
    return jax.shard_map(
        shards,
        mesh=mesh,
        in_specs=placed,
        out_specs=(P(("rows", "rep"), None), P(("rows", "rep"), None), P()),
        check_vma=False,
    )
```

profile of v0, /device:TPU:1, one launch (start us, length us, event | category | flops | bytes accessed | tf_op | source)
XLA Modules:
  0.0 688.1 jit_solution(9885065440772527485)
XLA Ops:
  12.0 75.1 %all-gather.3.cloned.1.call-done = bf16[16384,512]{1,0:T(8,128)(2,1)} async-done(((bf16[512,512]{1,0:T(8,128)(2,1)}), bf16[16384,512]{1,0:T(8,128)(2,1)}) %all-gather.3.cloned.1.call-update) | async-done | bytes 16777232 | tf_op jit(solution)/shard_map/all_gather | solution.py:43
  89.6 107.5 %while.10 = (s32[]{:T(128)}, f32[16,128,512]{2,1,0:T(8,128)}, s32[8,8]{1,0:T(8,128)S(1)}, bf16[8,8,128,128]{3,2,1,0:T(8,128)(2,1)}, s32[8,8]{1,0:T(8,128)S(1)}, /*index=5*/bf16[128,128,512]{2,1,0:T(8,128)(2,1)}, s32[]{:T(128)}) while((s32[]{:T(128)}, f32[16,128,512]{2,1,0:T(8,128)}, s32[8,8]{1,0:T(8,128)S(1)}, ...), condition=%wide.region_2.3_spmd, body=%wide.region_0.2_spmd.sunk | while | flops 134743088 | bytes 11800893 | solution.py:29
  89.6 7.4 %gather_fusion = bf16[8,128,512]{2,1,0:T(8,128)(2,1)} fusion(bf16[128,128,512]{2,1,0:T(8,128)(2,1)} %get-tuple-element.118, s32[1024]{0:T(1024)S(1)} %pad_clamp_fusion.3), kind=kCustom, calls=%fused_computation.clone.1 | custom fusion | bytes 2097184 | tf_op jit(solution)/shard_map/while/body/eval_jaxpr/gather | solution.py:18
  102.9 7.4 %gather_fusion = bf16[8,128,512]{2,1,0:T(8,128)(2,1)} fusion(bf16[128,128,512]{2,1,0:T(8,128)(2,1)} %get-tuple-element.118, s32[1024]{0:T(1024)S(1)} %pad_clamp_fusion.3), kind=kCustom, calls=%fused_computation.clone.1 | custom fusion | bytes 2097184 | tf_op jit(solution)/shard_map/while/body/eval_jaxpr/gather | solution.py:18
  116.2 7.4 %gather_fusion = bf16[8,128,512]{2,1,0:T(8,128)(2,1)} fusion(bf16[128,128,512]{2,1,0:T(8,128)(2,1)} %get-tuple-element.118, s32[1024]{0:T(1024)S(1)} %pad_clamp_fusion.3), kind=kCustom, calls=%fused_computation.clone.1 | custom fusion | bytes 2097184 | tf_op jit(solution)/shard_map/while/body/eval_jaxpr/gather | solution.py:18
  125.3 4.3 scatter_fusion
  129.6 7.4 %gather_fusion = bf16[8,128,512]{2,1,0:T(8,128)(2,1)} fusion(bf16[128,128,512]{2,1,0:T(8,128)(2,1)} %get-tuple-element.118, s32[1024]{0:T(1024)S(1)} %pad_clamp_fusion.3), kind=kCustom, calls=%fused_computation.clone.1 | custom fusion | bytes 2097184 | tf_op jit(solution)/shard_map/while/body/eval_jaxpr/gather | solution.py:18
  142.9 7.4 %gather_fusion = bf16[8,128,512]{2,1,0:T(8,128)(2,1)} fusion(bf16[128,128,512]{2,1,0:T(8,128)(2,1)} %get-tuple-element.118, s32[1024]{0:T(1024)S(1)} %pad_clamp_fusion.3), kind=kCustom, calls=%fused_computation.clone.1 | custom fusion | bytes 2097184 | tf_op jit(solution)/shard_map/while/body/eval_jaxpr/gather | solution.py:18
  152.0 4.5 scatter_fusion
  156.5 7.4 %gather_fusion = bf16[8,128,512]{2,1,0:T(8,128)(2,1)} fusion(bf16[128,128,512]{2,1,0:T(8,128)(2,1)} %get-tuple-element.118, s32[1024]{0:T(1024)S(1)} %pad_clamp_fusion.3), kind=kCustom, calls=%fused_computation.clone.1 | custom fusion | bytes 2097184 | tf_op jit(solution)/shard_map/while/body/eval_jaxpr/gather | solution.py:18
  165.5 4.5 scatter_fusion
  170.0 7.4 %gather_fusion = bf16[8,128,512]{2,1,0:T(8,128)(2,1)} fusion(bf16[128,128,512]{2,1,0:T(8,128)(2,1)} %get-tuple-element.118, s32[1024]{0:T(1024)S(1)} %pad_clamp_fusion.3), kind=kCustom, calls=%fused_computation.clone.1 | custom fusion | bytes 2097184 | tf_op jit(solution)/shard_map/while/body/eval_jaxpr/gather | solution.py:18
  179.1 4.5 scatter_fusion
  183.6 7.4 %gather_fusion = bf16[8,128,512]{2,1,0:T(8,128)(2,1)} fusion(bf16[128,128,512]{2,1,0:T(8,128)(2,1)} %get-tuple-element.118, s32[1024]{0:T(1024)S(1)} %pad_clamp_fusion.3), kind=kCustom, calls=%fused_computation.clone.1 | custom fusion | bytes 2097184 | tf_op jit(solution)/shard_map/while/body/eval_jaxpr/gather | solution.py:18
  192.7 4.5 scatter_fusion
  197.2 46.1 %reduce-scatter.3.cloned.1.call-done = f32[512,512]{1,0:T(8,128)} async-done(((f32[2048,512]{1,0:T(8,128)}), f32[512,512]{1,0:T(8,128)}) %reduce-scatter.3.cloned.1.call-update) | async-done | bytes 1048592 | tf_op jit(solution)/shard_map/reduce_scatter | solution.py:45
  246.2 30.4 %all-gather.5.cloned.1.call-done = bf16[2048,512]{1,0:T(8,128)(2,1)} async-done(((bf16[512,512]{1,0:T(8,128)(2,1)}), bf16[2048,512]{1,0:T(8,128)(2,1)}) %all-gather.5.cloned.1.call-update) | async-done | bytes 2097168 | tf_op jit(solution)/shard_map/all_gather | solution.py:51
  276.6 7.2 %gather_fusion.1 = bf16[64,128,512]{2,1,0:T(8,128)(2,1)} fusion(bf16[16,128,512]{2,1,0:T(8,128)(2,1)} %bitcast.45, s32[1024]{0:T(1024)S(1)} %pad_clamp_fusion.1), kind=kCustom, calls=%fused_computation.1 | custom fusion | bytes 16777472 | tf_op jit(solution)/shard_map/gather | solution.py:54
  283.8 11.5 %convolution_bitcast_fusion = f32[64,128,512]{1,2,0:T(8,128)} fusion(bf16[64,128,512]{2,1,0:T(8,128)(2,1)} %gather_fusion.1, bf16[64,128,128]{2,1,0:T(8,128)(2,1)S(1)} %bitcast.47), kind=kOutput, calls=%fused_computation.17 | convolution fusion | flops 1073741824 | bytes 27262976 | tf_op jit(solution)/shard_map/sji,sjf->sif/dot_general | solution.py:53
  295.4 17.5 %copy.14 = f32[64,128,512]{2,1,0:T(8,128)} copy(f32[64,128,512]{1,2,0:T(8,128)} %convolution_bitcast_fusion) | data formatting | bytes 33554432 | tf_op jit(solution)/shard_map/sji,sjf->sif/dot_general | solution.py:53
  312.8 11.3 %broadcast_in_dim.19 = f32[128,128,512]{2,1,0:T(8,128)} broadcast(f32[]{:T(128)} %constant.5.clone.1), dimensions={} | broadcast | bytes 33554436 | tf_op jit(solution)/shard_map/broadcast_in_dim | solution.py:58
  324.1 36.3 %scatter_fusion.1 = f32[128,128,512]{2,1,0:T(8,128)} fusion(f32[128,128,512]{2,1,0:T(8,128)} %broadcast_in_dim.19, s32[64]{0:T(128)S(1)} %compare_select_fusion.3, f32[64,128,512]{2,1,0:T(8,128)} %copy.14), kind=kCustom, calls=%fused_computation.3 | custom fusion | flops 4194304 | bytes 50331904 | tf_op jit(solution)/shard_map/scatter-add | solution.py:59
  360.4 165.6 %reduce-scatter.5.cloned.1.call-done = f32[512,512]{1,0:T(8,128)} async-done(((f32[16384,512]{1,0:T(8,128)}), f32[512,512]{1,0:T(8,128)}) %reduce-scatter.5.cloned.1.call-update) | async-done | bytes 1048592 | tf_op jit(solution)/shard_map/reduce_scatter | solution.py:60
  530.1 148.9 %all-reduce.2.cloned.1.call-done = f32[512,512]{0,1:T(8,128)} async-done(((f32[512,512]{0,1:T(8,128)}), f32[512,512]{0,1:T(8,128)}) %all-reduce.2.cloned.1.call-update) | async-done | bytes 1048592 | tf_op jit(solution)/shard_map/psum | solution.py:73
  (65 shorter events, 43.5 us)
Async XLA Ops:
  7.2 1.1 copy-start
  7.2 80.0 %all-gather.3.cloned.1.call-start = ((), (), s32[]{:S(2)}) async-start(), calls=%async_computation.2 | async-start | bytes 17301504 | tf_op jit(solution)/shard_map/all_gather | solution.py:43
  10.5 232.8 %reduce-scatter.3.cloned.1.call-start = ((), (), s32[]{:S(2)}) async-start(), calls=%async_computation.3 | async-start | bytes 5242880 | tf_op jit(solution)/shard_map/reduce_scatter | solution.py:45
  197.1 46.2 %copy-start.3 = (bf16[512,512]{1,0:T(8,128)(2,1)S(1)}, bf16[512,512]{1,0:T(8,128)(2,1)}, u32[]{:S(2)}) copy-start(bf16[512,512]{1,0:T(8,128)(2,1)} %param.17) | copy-start | bytes 1572868
  197.1 46.2 %copy-start.5 = (f32[512]{0:T(512)S(1)}, f32[512]{0:T(512)}, u32[]{:S(2)}) copy-start(f32[512]{0:T(512)} %param.12) | copy-start | bytes 6148
  197.1 49.0 %copy-start.6 = (s32[64]{0:T(128)S(1)}, s32[64]{0:T(128)}, u32[]{:S(2)}) copy-start(s32[64]{0:T(128)} %param.14) | copy-start | bytes 772
  197.1 49.1 %copy-start.7 = (s32[64]{0:T(128)S(1)}, s32[64]{0:T(128)}, u32[]{:S(2)}) copy-start(s32[64]{0:T(128)} %param.15) | copy-start | bytes 772
  197.2 79.5 %all-gather.5.cloned.1.call-start = ((), (), s32[]{:S(2)}) async-start(), calls=%async_computation.4 | async-start | bytes 2621440 | tf_op jit(solution)/shard_map/all_gather | solution.py:51
  246.1 279.9 %reduce-scatter.5.cloned.1.call-start = ((), (), s32[]{:S(2)}) async-start(), calls=%async_computation.5 | async-start | bytes 34603008 | tf_op jit(solution)/shard_map/reduce_scatter | solution.py:60
  276.6 7.2 %copy-start.1 = (bf16[8,8,128,128]{3,2,1,0:T(8,128)(2,1)S(1)}, bf16[8,8,128,128]{3,2,1,0:T(8,128)(2,1)}, u32[]{:S(2)}) copy-start(bf16[8,8,128,128]{3,2,1,0:T(8,128)(2,1)} %get-tuple-element.130) | copy-start | bytes 6291460
  360.3 168.5 %copy-start.4 = (bf16[512,512]{1,0:T(8,128)(2,1)S(1)}, bf16[512,512]{1,0:T(8,128)(2,1)}, u32[]{:S(2)}) copy-start(bf16[512,512]{1,0:T(8,128)(2,1)} %param.11) | copy-start | bytes 1572868
  360.4 318.6 %all-reduce.2.cloned.1.call-start = ((), (), s32[]{:S(2)}) async-start(), calls=%async_computation.6 | async-start | bytes 2097152 | tf_op jit(solution)/shard_map/psum | solution.py:73
  526.0 2.9 copy-start.2
Sparse Core Ops, SparseCore 0:
  10.8 76.2 all-gather.2
  197.3 45.9 reduce-scatter.2
  246.2 30.3 all-gather.4
  360.5 165.4 reduce-scatter.4
  531.2 147.7 all-reduce.1
where the time goes:
time: 689 us; the launch traced here: 688 us
  waiting for transfers between devices  466 us (68%)
  local copies, waits for them, and re-layouts  102 us (15%)
  other arithmetic  74.6 us (11%)
  matrix products  31.8 us (5%)
  between operations  13.9 us (2%)
    reduce_scatter x1, waiting for transfers between devices, shards(): lax.psum_scatter(totals.reshape(nodes_dev * lax.axis_size('rows'), feat_w...  166 us
    psum x1, waiting for transfers between devices, shards(): grad_weight = lax.psum(local_weight, ('rows', 'rep'))  149 us
    all_gather x1, waiting for transfers between devices, shards(): panels = lax.all_gather(scaled, 'rows', axis=0, tiled=True)  75.1 us
    gather x8, local copies, waits for them, and re-layouts, add_group(): panel_blocks[group_cols]  58.8 us
    reduce_scatter x1, waiting for transfers between devices, shards(): lax.psum_scatter(slab_part, 'rep', scatter_dimension=0, tiled=True)  46.1 us
    scatter-add x1, other arithmetic, shards(): totals = totals.at[target].add(products, mode='drop')  36.3 us
    scatter-add x8, other arithmetic, add_group(): return (totals.at[group_rows].add(products), None)  34.7 us
    all_gather x1, waiting for transfers between devices, shards(): slab_grads = lax.all_gather(scaled_grad, 'rep', axis=0, tiled=True)  30.4 us
  transfers between devices with their start and end apart: 5, of which 5 were waited for; matrix products, arithmetic and copies ran while one was open for 0% of the time, Pallas kernels for 0%

commit v1 on v0

v1 whole, which is shorter than its diff:
```python
import jax
import jax.numpy as jnp
from jax import lax
from jax.experimental import pallas as pl
from jax.experimental.pallas import tpu as pltpu
from jax.sharding import PartitionSpec as P


def _aggregate_kernel(rows_ref, cols_ref, tile_ref, panel_ref, out_ref):
    s = pl.program_id(0)

    @pl.when(s == 0)
    def _():
        out_ref[...] = jnp.zeros_like(out_ref)

    tile_size = tile_ref.shape[1]
    start = pl.multiple_of(rows_ref[s] * tile_size, tile_size)
    product = jnp.dot(tile_ref[0], panel_ref[...], preferred_element_type=jnp.float32)
    out_ref[pl.ds(start, tile_size), :] += product


def aggregate_slots(panels, group_rows, group_cols, tiles, out_blocks):
    slot_count, tile_size, _ = tiles.shape
    feat_width = panels.shape[1]
    grid_spec = pltpu.PrefetchScalarGridSpec(
        num_scalar_prefetch=2,
        grid=(slot_count,),
        in_specs=[
            pl.BlockSpec((1, tile_size, tile_size), lambda s, rows, cols: (s, 0, 0)),
            pl.BlockSpec((tile_size, feat_width), lambda s, rows, cols: (cols[s], 0)),
        ],
        out_specs=pl.BlockSpec((out_blocks * tile_size, feat_width), lambda s, rows, cols: (0, 0)),
    )
    return pl.pallas_call(
        _aggregate_kernel,
        grid_spec=grid_spec,
        out_shape=jax.ShapeDtypeStruct((out_blocks * tile_size, feat_width), jnp.float32),
        compiler_params=pltpu.CompilerParams(dimension_semantics=("arbitrary",)),
    )(group_rows, group_cols, tiles, panels)


def shards(features, weight, out_bias, degree, tile_row, tile_col, tile_value, cotangent):
    tile_size = tile_value.shape[1]
    nodes_dev = features.shape[0]
    block_count = nodes_dev // tile_size
    rep_count = lax.axis_size("rep")
    row_scale = lax.rsqrt(degree.astype(jnp.float32))[:, None]
    scaled = (jnp.dot(features, weight, preferred_element_type=jnp.float32) * row_scale).astype(
        jnp.bfloat16
    )
    panels = lax.all_gather(scaled, "rows", axis=0, tiled=True)
    slab_part = aggregate_slots(panels, tile_row, tile_col, tile_value, rep_count * block_count)
    aggregate = lax.psum_scatter(slab_part, "rep", scatter_dimension=0, tiled=True) * row_scale
    pre_act = aggregate + out_bias
    hidden_out = jax.nn.silu(pre_act).astype(jnp.bfloat16)
    sigmoid_pre = jax.nn.sigmoid(pre_act)
    grad_pre = cotangent.astype(jnp.float32) * sigmoid_pre * (1.0 + pre_act * (1.0 - sigmoid_pre))
    scaled_grad = (grad_pre * row_scale).astype(jnp.bfloat16)
    grad_panels = lax.all_gather(scaled_grad, "rows", axis=0, tiled=True)
    back_part = aggregate_slots(grad_panels, tile_row, tile_col, tile_value, rep_count * block_count)
    back_total = lax.psum_scatter(back_part, "rep", scatter_dimension=0, tiled=True)
    back_sum = (back_total * row_scale).astype(jnp.bfloat16)
    grad_input = lax.dot_general(
        back_sum, weight, (((1,), (1,)), ((), ())), preferred_element_type=jnp.float32
    ).astype(jnp.bfloat16)
    local_weight = lax.dot_general(
        features, back_sum, (((0,), (0,)), ((), ())), preferred_element_type=jnp.float32
    )
    grad_weight = lax.psum(local_weight, ("rows", "rep"))
    return (hidden_out, grad_input, grad_weight)


def solution(mesh):
    placed = (
        P(("rows", "rep"), None),
        P(),
        P(),
        P(("rows", "rep")),
        P(("rows", "rep")),
        P(("rows", "rep")),
        P(("rows", "rep"), None, None),
        P(("rows", "rep"), None),
    )
    return jax.shard_map(
        shards,
        mesh=mesh,
        in_specs=placed,
        out_specs=(P(("rows", "rep"), None), P(("rows", "rep"), None), P()),
        check_vma=False,
    )
```

time: 689 us -> 494 us (0.72)
  local copies, waits for them, and re-layouts: 102 us -> 2.82 us
  waiting for transfers between devices: 466 us -> 391 us
  Pallas kernels: 0 us -> 72.5 us
  other arithmetic: 74.6 us -> 3.52 us
  matrix products: 31.8 us -> 6.4 us
    reduce_scatter x1, waiting for transfers between devices: 166 us -> 46.1 us  [shards(): lax.psum_scatter(back_part, 'rep', scatter_dimension=0, tiled=True)]
    pallas_call x0 -> x2, Pallas kernels: none -> 72.5 us  [aggregate_slots(): pl.pallas_call(_aggregate_kernel, grid_spec=grid_spec, out_shape=jax.Shap...]
    scatter-add x9 -> x0, other arithmetic: 71 us -> none  [the longest x1 36.3 us: shards(): totals = totals.at[target].add(products, mode='drop')]
    gather x9 -> x0, local copies, waits for them, and re-layouts: 66 us -> none  [the longest x8 58.8 us: add_group(): panel_blocks[group_cols]]
    all_gather x1, waiting for transfers between devices: 30.4 us -> 73 us  [shards(): grad_panels = lax.all_gather(scaled_grad, 'rows', axis=0, tiled=True)]
    dot_general x9 -> x0, matrix products: 25.4 us -> none  [the longest x8 13.8 us: add_group(): jnp.einsum('sij,sjf->sif', group_tiles, panel_blocks[group_cols], preferr...]
    dot_general x1 -> x0, local copies, waits for them, and re-layouts: 17.5 us -> none  [shards(): jnp.einsum('sji,sjf->sif', tile_value, grad_blocks[tile_row], preferred_e...]
    broadcast_in_dim x2 -> x0, local copies, waits for them, and re-layouts: 13.7 us -> none  [the longest x1 11.3 us: shards(): totals = jnp.zeros((block_total, tile_size, feat_width), jnp.float32)]
where the time goes in v1:
time: 494 us; the launch traced here: 490 us
  waiting for transfers between devices  391 us (79%)
  Pallas kernels  72.5 us (15%)
  between operations  13.8 us (3%)
  matrix products  6.4 us (1%)
    psum x1, waiting for transfers between devices, shards(): grad_weight = lax.psum(local_weight, ('rows', 'rep'))  149 us
    all_gather x1, waiting for transfers between devices, shards(): panels = lax.all_gather(scaled, 'rows', axis=0, tiled=True)  76.6 us
    all_gather x1, waiting for transfers between devices, shards(): grad_panels = lax.all_gather(scaled_grad, 'rows', axis=0, tiled=True)  73 us
    pallas_call x2, Pallas kernels, aggregate_slots(): pl.pallas_call(_aggregate_kernel, grid_spec=grid_spec, out_shape=jax.Shap...  72.5 us
    reduce_scatter x1, waiting for transfers between devices, shards(): lax.psum_scatter(back_part, 'rep', scatter_dimension=0, tiled=True)  46.1 us
    reduce_scatter x1, waiting for transfers between devices, shards(): lax.psum_scatter(slab_part, 'rep', scatter_dimension=0, tiled=True)  46 us
  transfers between devices with their start and end apart: 5, of which 5 were waited for; matrix products, arithmetic and copies ran while one was open for 0% of the time, Pallas kernels for 0%

profile of v1, /device:TPU:1, one launch (start us, length us, event | category | flops | bytes accessed | tf_op | source)
XLA Modules:
  0.0 490.0 jit_solution(3218346082694402122)
XLA Ops:
  7.2 0.0 all-gather.3.cloned.1.call-start
  7.2 0.7 convert_rsqrt_fusion
  8.0 0.3 copy-done
  8.2 2.3 fusion
  10.5 0.0 all-gather.3.cloned.1.call-update
  10.5 0.0 reduce-scatter.3.cloned.1.call-start
  10.6 76.6 %all-gather.3.cloned.1.call-done.panel_ref = bf16[16384,512]{1,0:T(8,128)(2,1)} async-done(((bf16[512,512]{1,0:T(8,128)(2,1)}), bf16[16384,512]{1,0:T(8,128)(2,1)}) %all-gather.3.cloned.1.call-update) | async-done | bytes 16777232 | tf_op jit(solution)/shard_map/all_gather | solution.py:51
  87.1 36.2 %shard_map.103 = f32[2048,512]{1,0:T(8,128)} custom-call(s32[64]{0:T(128)} %rows_ref.3, s32[64]{0:T(128)} %cols_ref.3, bf16[64,128,128]{2,1,0:T(8,128)(2,1)} %tile_ref.3, bf16[16384,512]{1,0:T(8,128)(2,1)} %all-gather.3.cloned.1.call-done.panel_ref), custom_call_target="tpu_custom_call" | custom-call | tf_op jit(solution)/shard_map/pallas_call | solution.py:34
  123.4 0.0 reduce-scatter.3.cloned.1.call-update
  123.4 0.0 all-gather.5.cloned.1.call-start
  123.4 46.0 %reduce-scatter.3.cloned.1.call-done = f32[512,512]{1,0:T(8,128)} async-done(((f32[2048,512]{1,0:T(8,128)}), f32[512,512]{1,0:T(8,128)}) %reduce-scatter.3.cloned.1.call-update) | async-done | bytes 1048592 | tf_op jit(solution)/shard_map/reduce_scatter | solution.py:53
  169.5 2.8 multiply_convert_fusion.1
  172.3 0.0 all-gather.5.cloned.1.call-update
  172.3 0.0 reduce-scatter.5.cloned.1.call-start
  172.4 73.0 %all-gather.5.cloned.1.call-done.panel_ref = bf16[16384,512]{1,0:T(8,128)(2,1)} async-done(((bf16[512,512]{1,0:T(8,128)(2,1)}), bf16[16384,512]{1,0:T(8,128)(2,1)}) %all-gather.5.cloned.1.call-update) | async-done | bytes 16777232 | tf_op jit(solution)/shard_map/all_gather | solution.py:59
  245.3 36.2 %shard_map.104 = f32[2048,512]{1,0:T(8,128)} custom-call(s32[64]{0:T(128)} %rows_ref.3, s32[64]{0:T(128)} %cols_ref.3, bf16[64,128,128]{2,1,0:T(8,128)(2,1)} %tile_ref.3, bf16[16384,512]{1,0:T(8,128)(2,1)} %all-gather.5.cloned.1.call-done.panel_ref), custom_call_target="tpu_custom_call" | custom-call | tf_op jit(solution)/shard_map/pallas_call | solution.py:34
  281.6 0.0 reduce-scatter.5.cloned.1.call-update
  281.6 0.0 all-reduce.2.cloned.1.call-start
  281.6 46.1 %reduce-scatter.5.cloned.1.call-done = f32[512,512]{1,0:T(8,128)} async-done(((f32[2048,512]{1,0:T(8,128)}), f32[512,512]{1,0:T(8,128)}) %reduce-scatter.5.cloned.1.call-update) | async-done | bytes 1048592 | tf_op jit(solution)/shard_map/reduce_scatter | solution.py:61
  327.7 2.8 convolution_bitcast_fusion
  330.5 0.0 all-reduce.2.cloned.1.call-update
  330.6 1.3 convolution_convert_fusion
  331.9 149.1 %all-reduce.2.cloned.1.call-done = f32[512,512]{0,1:T(8,128)} async-done(((f32[512,512]{0,1:T(8,128)}), f32[512,512]{0,1:T(8,128)}) %all-reduce.2.cloned.1.call-update) | async-done | bytes 1048592 | tf_op jit(solution)/shard_map/psum | solution.py:69
  481.0 2.5 copy.11
  (9 shorter events, 0.0 us)
Async XLA Ops:
  7.2 1.1 copy-start
  7.2 80.0 %all-gather.3.cloned.1.call-start = ((), (), s32[]{:S(2)}) async-start(), calls=%async_computation.2 | async-start | bytes 17301504 | tf_op jit(solution)/shard_map/all_gather | solution.py:51
  10.5 159.0 %reduce-scatter.3.cloned.1.call-start = ((), (), s32[]{:S(2)}) async-start(), calls=%async_computation.3 | async-start | bytes 5242880 | tf_op jit(solution)/shard_map/reduce_scatter | solution.py:53
  123.4 46.1 %copy-start.2 = (bf16[512,512]{1,0:T(8,128)(2,1)S(1)}, bf16[512,512]{1,0:T(8,128)(2,1)}, u32[]{:S(2)}) copy-start(bf16[512,512]{1,0:T(8,128)(2,1)} %param.15) | copy-start | bytes 1572868
  123.4 46.1 %copy-start.4 = (f32[512]{0:T(512)S(1)}, f32[512]{0:T(512)}, u32[]{:S(2)}) copy-start(f32[512]{0:T(512)} %param.10) | copy-start | bytes 6148
  123.4 121.9 %all-gather.5.cloned.1.call-start = ((), (), s32[]{:S(2)}) async-start(), calls=%async_computation.4 | async-start | bytes 17301504 | tf_op jit(solution)/shard_map/all_gather | solution.py:59
  172.3 155.4 %reduce-scatter.5.cloned.1.call-start = ((), (), s32[]{:S(2)}) async-start(), calls=%async_computation.5 | async-start | bytes 5242880 | tf_op jit(solution)/shard_map/reduce_scatter | solution.py:61
  281.6 49.0 %copy-start.3 = (bf16[512,512]{1,0:T(8,128)(2,1)S(1)}, bf16[512,512]{1,0:T(8,128)(2,1)}, u32[]{:S(2)}) copy-start(bf16[512,512]{1,0:T(8,128)(2,1)} %param.9) | copy-start | bytes 1572868
  281.6 199.4 %all-reduce.2.cloned.1.call-start = ((), (), s32[]{:S(2)}) async-start(), calls=%async_computation.6 | async-start | bytes 2097152 | tf_op jit(solution)/shard_map/psum | solution.py:69
  327.7 2.9 copy-start.1
Sparse Core Ops, SparseCore 0:
  10.8 76.2 all-gather.2
  123.5 45.9 reduce-scatter.2
  172.4 72.8 all-gather.4
  281.7 45.9 reduce-scatter.4
  332.9 148.0 all-reduce.1

commit v2 on v1

--- a/solution.py
+++ b/solution.py
@@ -39,6 +39,17 @@
     )(group_rows, group_cols, tiles, panels)
 
 
+def all_reduce_by_exchange(value, axes):
+    count = 1
+    for axis in axes:
+        count *= lax.axis_size(axis)
+    rows, width = value.shape
+    chunks = lax.all_to_all(value.reshape(count, rows // count, width), axes, 0, 0, tiled=True)
+    own = chunks.sum(axis=0)
+    spread = jnp.broadcast_to(own[None], (count,) + own.shape)
+    return lax.all_to_all(spread, axes, 0, 0, tiled=True).reshape(rows, width)
+
+
 def shards(features, weight, out_bias, degree, tile_row, tile_col, tile_value, cotangent):
     tile_size = tile_value.shape[1]
     nodes_dev = features.shape[0]
@@ -66,7 +77,7 @@
     local_weight = lax.dot_general(
         features, back_sum, (((0,), (0,)), ((), ())), preferred_element_type=jnp.float32
     )
-    grad_weight = lax.psum(local_weight, ("rows", "rep"))
+    grad_weight = all_reduce_by_exchange(local_weight, ("rows", "rep"))
     return (hidden_out, grad_input, grad_weight)
 
 

time: 494 us -> 400 us (0.81)
  waiting for transfers between devices: 391 us -> 264 us
  blocking collectives: 0 us -> 27.4 us
    psum x1 -> x0, waiting for transfers between devices: 149 us -> none  [shards(): grad_weight = lax.psum(local_weight, ('rows', 'rep'))]
    all_to_all x0 -> x1, blocking collectives: none -> 27.4 us  [all_reduce_by_exchange(): lax.all_to_all(value.reshape(count, rows // count, width), axes, 0, 0, ti...]
    all_to_all x0 -> x1, waiting for transfers between devices: none -> 18.1 us  [all_reduce_by_exchange(): return lax.all_to_all(spread, axes, 0, 0, tiled=True).reshape(rows, width)]
where the time goes in v2:
time: 400 us; the launch traced here: 396 us
  waiting for transfers between devices  264 us (66%)
  Pallas kernels  73.7 us (18%)
  blocking collectives  27.4 us (7%)
  between operations  13.8 us (3%)
  matrix products  5.3 us (1%)
  starting transfers between devices  4.07 us (1%)
  local copies, waits for them, and re-layouts  4.01 us (1%)
    all_gather x1, waiting for transfers between devices, shards(): panels = lax.all_gather(scaled, 'rows', axis=0, tiled=True)  76.6 us
    pallas_call x2, Pallas kernels, aggregate_slots(): pl.pallas_call(_aggregate_kernel, grid_spec=grid_spec, out_shape=jax.Shap...  73.7 us
    all_gather x1, waiting for transfers between devices, shards(): grad_panels = lax.all_gather(scaled_grad, 'rows', axis=0, tiled=True)  73 us
    reduce_scatter x1, waiting for transfers between devices, shards(): lax.psum_scatter(back_part, 'rep', scatter_dimension=0, tiled=True)  48.1 us
    reduce_scatter x1, waiting for transfers between devices, shards(): lax.psum_scatter(slab_part, 'rep', scatter_dimension=0, tiled=True)  48 us
    all_to_all x1, blocking collectives, all_reduce_by_exchange(): lax.all_to_all(value.reshape(count, rows // count, width), axes, 0, 0, ti...  27.4 us
    all_to_all x1, waiting for transfers between devices, all_reduce_by_exchange(): return lax.all_to_all(spread, axes, 0, 0, tiled=True).reshape(rows, width)  18.1 us
  transfers between devices with their start and end apart: 5, of which 5 were waited for; matrix products, arithmetic and copies ran while one was open for 0% of the time, Pallas kernels for 0%

profile of v2, /device:TPU:1, one launch (start us, length us, event | category | flops | bytes accessed | tf_op | source)
XLA Modules:
  0.0 395.8 jit_solution(3321532521730977334)
XLA Ops:
  7.2 0.0 all-gather.3.cloned.1.call-start
  7.2 0.7 convert_rsqrt_fusion
  8.0 0.3 copy-done
  8.2 2.3 fusion
  10.5 0.0 reduce-scatter.3.cloned.1.call-start
  10.6 76.6 %all-gather.3.cloned.1.call-done.panel_ref = bf16[16384,512]{1,0:T(8,128)(2,1)} async-done(((bf16[512,512]{1,0:T(8,128)(2,1)}), bf16[16384,512]{1,0:T(8,128)(2,1)}) %all-gather.3.cloned.1.call-update) | async-done | bytes 16777232 | tf_op jit(solution)/shard_map/all_gather | solution.py:62
  87.1 36.9 %shard_map.103 = f32[2048,512]{1,0:T(8,128)} custom-call(s32[64]{0:T(128)} %rows_ref.3, s32[64]{0:T(128)} %cols_ref.3, bf16[64,128,128]{2,1,0:T(8,128)(2,1)} %tile_ref.3, bf16[16384,512]{1,0:T(8,128)(2,1)} %all-gather.3.cloned.1.call-done.panel_ref), custom_call_target="tpu_custom_call" | custom-call | tf_op jit(solution)/shard_map/pallas_call | solution.py:34
  124.0 0.0 all-gather.5.cloned.1.call-start
  124.1 48.0 %reduce-scatter.3.cloned.1.call-done = f32[512,512]{1,0:T(8,128)} async-done(((f32[2048,512]{1,0:T(8,128)}), f32[512,512]{1,0:T(8,128)}) %reduce-scatter.3.cloned.1.call-update) | async-done | bytes 1048592 | tf_op jit(solution)/shard_map/reduce_scatter | solution.py:64
  172.1 2.8 multiply_convert_fusion.1
  174.9 0.0 all-gather.5.cloned.1.call-update
  174.9 0.0 reduce-scatter.5.cloned.1.call-start
  175.0 73.0 %all-gather.5.cloned.1.call-done.panel_ref = bf16[16384,512]{1,0:T(8,128)(2,1)} async-done(((bf16[512,512]{1,0:T(8,128)(2,1)}), bf16[16384,512]{1,0:T(8,128)(2,1)}) %all-gather.5.cloned.1.call-update) | async-done | bytes 16777232 | tf_op jit(solution)/shard_map/all_gather | solution.py:70
  247.9 36.9 %shard_map.104 = f32[2048,512]{1,0:T(8,128)} custom-call(s32[64]{0:T(128)} %rows_ref.3, s32[64]{0:T(128)} %cols_ref.3, bf16[64,128,128]{2,1,0:T(8,128)(2,1)} %tile_ref.3, bf16[16384,512]{1,0:T(8,128)(2,1)} %all-gather.5.cloned.1.call-done.panel_ref), custom_call_target="tpu_custom_call" | custom-call | tf_op jit(solution)/shard_map/pallas_call | solution.py:34
  284.8 48.1 %reduce-scatter.5.cloned.1.call-done = f32[512,512]{1,0:T(8,128)} async-done(((f32[2048,512]{1,0:T(8,128)}), f32[512,512]{1,0:T(8,128)}) %reduce-scatter.5.cloned.1.call-update) | async-done | bytes 1048592 | tf_op jit(solution)/shard_map/reduce_scatter | solution.py:72
  333.0 1.7 convolution_bitcast_fusion
  334.7 1.3 reshape.15
  336.0 27.4 %all_to_all.10 = f32[128,4,512]{2,1,0:T(4,128)S(1)} all-to-all(f32[128,4,512]{2,1,0:T(4,128)} %reshape.15), channel_id=1, replica_groups=mesh['rows'=32,'rep'=4] {'rows','rep'}, dimensions={0} | all-to-all | bytes 2097152 | tf_op jit(solution)/shard_map/all_to_all | solution.py:47
  363.4 0.2 reduce_sum.9
  363.6 1.1 broadcast_in_dim.2
  364.7 3.9 all-to-all-start.1
  368.6 1.3 convolution_convert_fusion
  369.9 18.1 %all-to-all-done.1 = f32[128,4,512]{2,1,0:T(4,128)S(1)} async-done(((f32[128,4,512]{2,1,0:T(4,128)}), f32[128,4,512]{2,1,0:T(4,128)S(1)}, u32[]{:S(2)}, u32[]{:S(2)}) %all-to-all-start.1) | async-done | bytes 1048608 | tf_op jit(solution)/shard_map/all_to_all | solution.py:50
  388.0 1.3 reshape.16
  (12 shorter events, 0.1 us)
Async XLA Ops:
  7.2 1.1 copy-start
  7.2 80.0 %all-gather.3.cloned.1.call-start = ((), (), s32[]{:S(2)}) async-start(), calls=%async_computation.4 | async-start | bytes 17301504 | tf_op jit(solution)/shard_map/all_gather | solution.py:62
  10.5 161.6 %reduce-scatter.3.cloned.1.call-start = ((), (), s32[]{:S(2)}) async-start(), calls=%async_computation.5 | async-start | bytes 5242880 | tf_op jit(solution)/shard_map/reduce_scatter | solution.py:64
  124.0 48.1 %copy-start.2 = (bf16[512,512]{1,0:T(8,128)(2,1)S(1)}, bf16[512,512]{1,0:T(8,128)(2,1)}, u32[]{:S(2)}) copy-start(bf16[512,512]{1,0:T(8,128)(2,1)} %param.15) | copy-start | bytes 1572868
  124.0 48.1 %copy-start.4 = (f32[512]{0:T(512)S(1)}, f32[512]{0:T(512)}, u32[]{:S(2)}) copy-start(f32[512]{0:T(512)} %param.10) | copy-start | bytes 6148
  124.0 123.9 %all-gather.5.cloned.1.call-start = ((), (), s32[]{:S(2)}) async-start(), calls=%async_computation.6 | async-start | bytes 17301504 | tf_op jit(solution)/shard_map/all_gather | solution.py:70
  174.9 158.0 %reduce-scatter.5.cloned.1.call-start = ((), (), s32[]{:S(2)}) async-start(), calls=%async_computation.7 | async-start | bytes 5242880 | tf_op jit(solution)/shard_map/reduce_scatter | solution.py:72
  334.7 33.9 %copy-start.1 = (f32[512,512]{1,0:T(8,128)S(1)}, f32[512,512]{1,0:T(8,128)}, u32[]{:S(2)}) copy-start(f32[512,512]{1,0:T(8,128)} %reduce-scatter.5.cloned.1.call-done) | copy-start | bytes 3145732
  334.7 33.9 %copy-start.3 = (bf16[512,512]{1,0:T(8,128)(2,1)S(1)}, bf16[512,512]{1,0:T(8,128)(2,1)}, u32[]{:S(2)}) copy-start(bf16[512,512]{1,0:T(8,128)(2,1)} %param.9) | copy-start | bytes 1572868
  364.7 23.3 %all-to-all-start.1 = ((f32[128,4,512]{2,1,0:T(4,128)}), f32[128,4,512]{2,1,0:T(4,128)S(1)}, u32[]{:S(2)}, u32[]{:S(2)}) async-start(f32[128,4,512]{2,1,0:T(4,128)} %broadcast_in_dim.2), calls=%async_computation.3 | async-start | bytes 2097152 | tf_op jit(solution)/shard_map/all_to_all | solution.py:50
Sparse Core Ops, SparseCore 0:
  10.8 76.2 all-gather.2
  124.2 47.8 reduce-scatter.2
  175.0 72.8 all-gather.4
  285.0 47.9 reduce-scatter.4

commit v3 on v2

--- a/solution.py
+++ b/solution.py
@@ -6,17 +6,40 @@
 from jax.sharding import PartitionSpec as P
 
 
-def _aggregate_kernel(rows_ref, cols_ref, tile_ref, panel_ref, out_ref):
-    s = pl.program_id(0)
+PANEL_BUFFERS = 4
 
-    @pl.when(s == 0)
-    def _():
-        out_ref[...] = jnp.zeros_like(out_ref)
 
-    tile_size = tile_ref.shape[1]
-    start = pl.multiple_of(rows_ref[s] * tile_size, tile_size)
-    product = jnp.dot(tile_ref[0], panel_ref[...], preferred_element_type=jnp.float32)
-    out_ref[pl.ds(start, tile_size), :] += product
+def _aggregate_kernel(rows_ref, cols_ref, tiles_ref, panels_hbm, out_ref, buffers, sems):
+    slot_count, tile_size, _ = tiles_ref.shape
+    panel_blocks = panels_hbm.shape[0] // tile_size
+    out_blocks = out_ref.shape[0] // tile_size
+
+    def panel_copy(s, buffer):
+        col = jnp.clip(cols_ref[s], 0, panel_blocks - 1)
+        start = pl.multiple_of(col * tile_size, tile_size)
+        return pltpu.make_async_copy(
+            panels_hbm.at[pl.ds(start, tile_size), :], buffers.at[buffer], sems.at[buffer]
+        )
+
+    for buffer in range(PANEL_BUFFERS):
+        panel_copy(buffer, buffer).start()
+    out_ref[...] = jnp.zeros_like(out_ref)
+
+    def step(s, carry):
+        buffer = s % PANEL_BUFFERS
+        panel_copy(s, buffer).wait()
+        row = jnp.clip(rows_ref[s], 0, out_blocks - 1)
+        start = pl.multiple_of(row * tile_size, tile_size)
+        product = jnp.dot(tiles_ref[s], buffers[buffer], preferred_element_type=jnp.float32)
+        out_ref[pl.ds(start, tile_size), :] += product
+
+        @pl.when(s + PANEL_BUFFERS < slot_count)
+        def _():
+            panel_copy(s + PANEL_BUFFERS, buffer).start()
+
+        return carry
+
+    lax.fori_loop(0, slot_count, step, 0)
 
 
 def aggregate_slots(panels, group_rows, group_cols, tiles, out_blocks):
@@ -24,12 +47,16 @@
     feat_width = panels.shape[1]
     grid_spec = pltpu.PrefetchScalarGridSpec(
         num_scalar_prefetch=2,
-        grid=(slot_count,),
+        grid=(1,),
         in_specs=[
-            pl.BlockSpec((1, tile_size, tile_size), lambda s, rows, cols: (s, 0, 0)),
-            pl.BlockSpec((tile_size, feat_width), lambda s, rows, cols: (cols[s], 0)),
+            pl.BlockSpec((slot_count, tile_size, tile_size), lambda i, rows, cols: (0, 0, 0)),
+            pl.BlockSpec(memory_space=pl.ANY),
         ],
-        out_specs=pl.BlockSpec((out_blocks * tile_size, feat_width), lambda s, rows, cols: (0, 0)),
+        out_specs=pl.BlockSpec((out_blocks * tile_size, feat_width), lambda i, rows, cols: (0, 0)),
+        scratch_shapes=[
+            pltpu.VMEM((PANEL_BUFFERS, tile_size, feat_width), panels.dtype),
+            pltpu.SemaphoreType.DMA((PANEL_BUFFERS,)),
+        ],
     )
     return pl.pallas_call(
         _aggregate_kernel,

time: 400 us -> 359 us (0.90)
  Pallas kernels: 73.7 us -> 40.6 us
  waiting for transfers between devices: 264 us -> 259 us
    pallas_call x2, Pallas kernels: 73.7 us -> 40.6 us  [aggregate_slots(): pl.pallas_call(_aggregate_kernel, grid_spec=grid_spec, out_shape=jax.Shap...]
where the time goes in v3:
time: 359 us; the launch traced here: 358 us
  waiting for transfers between devices  259 us (72%)
  Pallas kernels  40.6 us (11%)
  blocking collectives  27.4 us (8%)
  between operations  13.9 us (4%)
  matrix products  5.31 us (1%)
  starting transfers between devices  4.07 us (1%)
  local copies, waits for them, and re-layouts  4.01 us (1%)
  other arithmetic  3.73 us (1%)
    all_gather x1, waiting for transfers between devices, shards(): panels = lax.all_gather(scaled, 'rows', axis=0, tiled=True)  76.6 us
    all_gather x1, waiting for transfers between devices, shards(): grad_panels = lax.all_gather(scaled_grad, 'rows', axis=0, tiled=True)  73 us
    reduce_scatter x1, waiting for transfers between devices, shards(): lax.psum_scatter(back_part, 'rep', scatter_dimension=0, tiled=True)  45.9 us
    reduce_scatter x1, waiting for transfers between devices, shards(): lax.psum_scatter(slab_part, 'rep', scatter_dimension=0, tiled=True)  45.9 us
    pallas_call x2, Pallas kernels, aggregate_slots(): pl.pallas_call(_aggregate_kernel, grid_spec=grid_spec, out_shape=jax.Shap...  40.6 us
    all_to_all x1, blocking collectives, all_reduce_by_exchange(): lax.all_to_all(value.reshape(count, rows // count, width), axes, 0, 0, ti...  27.4 us
    all_to_all x1, waiting for transfers between devices, all_reduce_by_exchange(): return lax.all_to_all(spread, axes, 0, 0, tiled=True).reshape(rows, width)  18 us
  transfers between devices with their start and end apart: 5, of which 5 were waited for; matrix products, arithmetic and copies ran while one was open for 0% of the time, Pallas kernels for 0%

profile of v3, /device:TPU:1, one launch (start us, length us, event | category | flops | bytes accessed | tf_op | source)
XLA Modules:
  0.0 358.4 jit_solution(8334405442258102128)
XLA Ops:
  7.2 0.0 all-gather.3.cloned.1.call-start
  7.2 0.7 convert_rsqrt_fusion
  8.0 0.3 copy-done
  8.2 2.3 fusion
  10.5 0.0 reduce-scatter.3.cloned.1.call-start
  10.6 76.6 %all-gather.3.cloned.1.call-done.panels_hbm = bf16[16384,512]{1,0:T(8,128)(2,1)} async-done(((bf16[512,512]{1,0:T(8,128)(2,1)}), bf16[16384,512]{1,0:T(8,128)(2,1)}) %all-gather.3.cloned.1.call-update) | async-done | bytes 16777232 | tf_op jit(solution)/shard_map/all_gather | solution.py:89
  87.1 20.3 %shard_map.103 = f32[2048,512]{1,0:T(8,128)} custom-call(s32[64]{0:T(128)} %rows_ref.3, s32[64]{0:T(128)} %cols_ref.3, bf16[64,128,128]{2,1,0:T(8,128)(2,1)} %tiles_ref.3, bf16[16384,512]{1,0:T(8,128)(2,1)} %all-gather.3.cloned.1.call-done.panels_hbm), custom_call_target="tpu_custom_call" | custom-call | tf_op jit(solution)/shard_map/pallas_call | solution.py:61
  107.5 0.0 reduce-scatter.3.cloned.1.call-update
  107.5 0.0 all-gather.5.cloned.1.call-start
  107.5 45.9 %reduce-scatter.3.cloned.1.call-done = f32[512,512]{1,0:T(8,128)} async-done(((f32[2048,512]{1,0:T(8,128)}), f32[512,512]{1,0:T(8,128)}) %reduce-scatter.3.cloned.1.call-update) | async-done | bytes 1048592 | tf_op jit(solution)/shard_map/reduce_scatter | solution.py:91
  153.4 2.8 multiply_convert_fusion.1
  156.2 0.0 reduce-scatter.5.cloned.1.call-start
  156.3 73.0 %all-gather.5.cloned.1.call-done.panels_hbm = bf16[16384,512]{1,0:T(8,128)(2,1)} async-done(((bf16[512,512]{1,0:T(8,128)(2,1)}), bf16[16384,512]{1,0:T(8,128)(2,1)}) %all-gather.5.cloned.1.call-update) | async-done | bytes 16777232 | tf_op jit(solution)/shard_map/all_gather | solution.py:97
  229.3 20.3 %shard_map.104 = f32[2048,512]{1,0:T(8,128)} custom-call(s32[64]{0:T(128)} %rows_ref.3, s32[64]{0:T(128)} %cols_ref.3, bf16[64,128,128]{2,1,0:T(8,128)(2,1)} %tiles_ref.3, bf16[16384,512]{1,0:T(8,128)(2,1)} %all-gather.5.cloned.1.call-done.panels_hbm), custom_call_target="tpu_custom_call" | custom-call | tf_op jit(solution)/shard_map/pallas_call | solution.py:61
  249.6 45.9 %reduce-scatter.5.cloned.1.call-done = f32[512,512]{1,0:T(8,128)} async-done(((f32[2048,512]{1,0:T(8,128)}), f32[512,512]{1,0:T(8,128)}) %reduce-scatter.5.cloned.1.call-update) | async-done | bytes 1048592 | tf_op jit(solution)/shard_map/reduce_scatter | solution.py:99
  295.5 1.7 convolution_bitcast_fusion
  297.3 1.3 reshape.15
  298.6 27.4 %all_to_all.10 = f32[128,4,512]{2,1,0:T(4,128)S(1)} all-to-all(f32[128,4,512]{2,1,0:T(4,128)} %reshape.15), channel_id=1, replica_groups=mesh['rows'=32,'rep'=4] {'rows','rep'}, dimensions={0} | all-to-all | bytes 2097152 | tf_op jit(solution)/shard_map/all_to_all | solution.py:74
  325.9 0.2 reduce_sum.9
  326.1 1.1 broadcast_in_dim.2
  327.3 3.9 %all-to-all-start.1 = ((f32[128,4,512]{2,1,0:T(4,128)}), f32[128,4,512]{2,1,0:T(4,128)S(1)}, u32[]{:S(2)}, u32[]{:S(2)}) async-start(f32[128,4,512]{2,1,0:T(4,128)} %broadcast_in_dim.2), calls=%async_computation.3 | async-start | bytes 2097152 | tf_op jit(solution)/shard_map/all_to_all | solution.py:77
  331.2 1.3 convolution_convert_fusion
  332.5 18.0 %all-to-all-done.1 = f32[128,4,512]{2,1,0:T(4,128)S(1)} async-done(((f32[128,4,512]{2,1,0:T(4,128)}), f32[128,4,512]{2,1,0:T(4,128)S(1)}, u32[]{:S(2)}, u32[]{:S(2)}) %all-to-all-start.1) | async-done | bytes 1048608 | tf_op jit(solution)/shard_map/all_to_all | solution.py:77
  350.5 1.3 reshape.16
  (12 shorter events, 0.1 us)
Async XLA Ops:
  7.2 1.1 copy-start
  7.2 80.0 %all-gather.3.cloned.1.call-start = ((), (), s32[]{:S(2)}) async-start(), calls=%async_computation.4 | async-start | bytes 17301504 | tf_op jit(solution)/shard_map/all_gather | solution.py:89
  10.5 142.9 %reduce-scatter.3.cloned.1.call-start = ((), (), s32[]{:S(2)}) async-start(), calls=%async_computation.5 | async-start | bytes 5242880 | tf_op jit(solution)/shard_map/reduce_scatter | solution.py:91
  107.5 46.0 %copy-start.2 = (bf16[512,512]{1,0:T(8,128)(2,1)S(1)}, bf16[512,512]{1,0:T(8,128)(2,1)}, u32[]{:S(2)}) copy-start(bf16[512,512]{1,0:T(8,128)(2,1)} %param.15) | copy-start | bytes 1572868
  107.5 46.0 %copy-start.4 = (f32[512]{0:T(512)S(1)}, f32[512]{0:T(512)}, u32[]{:S(2)}) copy-start(f32[512]{0:T(512)} %param.10) | copy-start | bytes 6148
  107.5 121.8 %all-gather.5.cloned.1.call-start = ((), (), s32[]{:S(2)}) async-start(), calls=%async_computation.6 | async-start | bytes 17301504 | tf_op jit(solution)/shard_map/all_gather | solution.py:97
  156.2 139.3 %reduce-scatter.5.cloned.1.call-start = ((), (), s32[]{:S(2)}) async-start(), calls=%async_computation.7 | async-start | bytes 5242880 | tf_op jit(solution)/shard_map/reduce_scatter | solution.py:99
  297.3 33.9 %copy-start.1 = (f32[512,512]{1,0:T(8,128)S(1)}, f32[512,512]{1,0:T(8,128)}, u32[]{:S(2)}) copy-start(f32[512,512]{1,0:T(8,128)} %reduce-scatter.5.cloned.1.call-done) | copy-start | bytes 3145732
  297.3 33.9 %copy-start.3 = (bf16[512,512]{1,0:T(8,128)(2,1)S(1)}, bf16[512,512]{1,0:T(8,128)(2,1)}, u32[]{:S(2)}) copy-start(bf16[512,512]{1,0:T(8,128)(2,1)} %param.9) | copy-start | bytes 1572868
  327.3 23.3 %all-to-all-start.1 = ((f32[128,4,512]{2,1,0:T(4,128)}), f32[128,4,512]{2,1,0:T(4,128)S(1)}, u32[]{:S(2)}, u32[]{:S(2)}) async-start(f32[128,4,512]{2,1,0:T(4,128)} %broadcast_in_dim.2), calls=%async_computation.3 | async-start | bytes 2097152 | tf_op jit(solution)/shard_map/all_to_all | solution.py:77
Sparse Core Ops, SparseCore 0:
  10.8 76.2 all-gather.2
  107.6 45.7 reduce-scatter.2
  156.4 72.8 all-gather.4
  249.7 45.7 reduce-scatter.4

commit v4 on v3

--- a/solution.py
+++ b/solution.py
@@ -77,6 +77,12 @@
     return lax.all_to_all(spread, axes, 0, 0, tiled=True).reshape(rows, width)
 
 
+def gather_by_exchange(value, axis):
+    count = lax.axis_size(axis)
+    copies = jnp.broadcast_to(value[None], (count,) + value.shape)
+    return lax.all_to_all(copies, axis, 0, 0, tiled=True).reshape((-1,) + value.shape[1:])
+
+
 def shards(features, weight, out_bias, degree, tile_row, tile_col, tile_value, cotangent):
     tile_size = tile_value.shape[1]
     nodes_dev = features.shape[0]
@@ -87,6 +93,8 @@
         jnp.bfloat16
     )
     panels = lax.all_gather(scaled, "rows", axis=0, tiled=True)
+    slab_features = gather_by_exchange(features, "rep")
+    slab_scale = gather_by_exchange(row_scale, "rep")
     slab_part = aggregate_slots(panels, tile_row, tile_col, tile_value, rep_count * block_count)
     aggregate = lax.psum_scatter(slab_part, "rep", scatter_dimension=0, tiled=True) * row_scale
     pre_act = aggregate + out_bias
@@ -102,7 +110,7 @@
         back_sum, weight, (((1,), (1,)), ((), ())), preferred_element_type=jnp.float32
     ).astype(jnp.bfloat16)
     local_weight = lax.dot_general(
-        features, back_sum, (((0,), (0,)), ((), ())), preferred_element_type=jnp.float32
+        slab_features, back_part * slab_scale, (((0,), (0,)), ((), ())), preferred_element_type=jnp.float32
     )
     grad_weight = all_reduce_by_exchange(local_weight, ("rows", "rep"))
     return (hidden_out, grad_input, grad_weight)

time: 359 us -> 373 us (1.039)
  blocking collectives: 27.4 us -> 109 us
  waiting for transfers between devices: 259 us -> 195 us
  starting transfers between devices: 4.07 us -> 0.16 us
    all_to_all x0 -> x3, blocking collectives: none -> 82.4 us  [the longest x2 59.4 us: gather_by_exchange(): lax.all_to_all(copies, axis, 0, 0, tiled=True)]
    reduce_scatter x1, waiting for transfers between devices: 45.9 us -> 0.01 us  [shards(): lax.psum_scatter(back_part, 'rep', scatter_dimension=0, tiled=True)]
    all_to_all x1 -> x0, waiting for transfers between devices: 18 us -> none  [all_reduce_by_exchange(): return lax.all_to_all(spread, axes, 0, 0, tiled=True).reshape(rows, width)]
    all_to_all x1 -> x0, starting transfers between devices: 3.91 us -> none  [all_reduce_by_exchange(): return lax.all_to_all(spread, axes, 0, 0, tiled=True).reshape(rows, width)]
  transfers between devices with their start and end apart: 5 -> 4, of which waited for: 5 -> 3; matrix products, arithmetic and copies ran while one was open for 0% -> 1% of each run, Pallas kernels for 0% -> 0%
where the time goes in v4:
time: 373 us; the launch traced here: 372 us
  waiting for transfers between devices  195 us (52%)
  blocking collectives  109 us (29%)
  Pallas kernels  40.6 us (11%)
  between operations  13.9 us (4%)
  matrix products  6.23 us (2%)
  other arithmetic  3.73 us (1%)
    all_gather x1, waiting for transfers between devices, shards(): panels = lax.all_gather(scaled, 'rows', axis=0, tiled=True)  76.6 us
    all_gather x1, waiting for transfers between devices, shards(): grad_panels = lax.all_gather(scaled_grad, 'rows', axis=0, tiled=True)  73 us
    all_to_all x2, blocking collectives, gather_by_exchange(): lax.all_to_all(copies, axis, 0, 0, tiled=True)  59.4 us
    reduce_scatter x1, waiting for transfers between devices, shards(): lax.psum_scatter(slab_part, 'rep', scatter_dimension=0, tiled=True)  45.9 us
    pallas_call x2, Pallas kernels, aggregate_slots(): pl.pallas_call(_aggregate_kernel, grid_spec=grid_spec, out_shape=jax.Shap...  40.6 us
    all_to_all x1, blocking collectives, all_reduce_by_exchange(): lax.all_to_all(value.reshape(count, rows // count, width), axes, 0, 0, ti...  26.8 us
    all_to_all x1, blocking collectives, all_reduce_by_exchange(): return lax.all_to_all(spread, axes, 0, 0, tiled=True).reshape(rows, width)  23 us
  transfers between devices with their start and end apart: 4, of which 3 were waited for; matrix products, arithmetic and copies ran while one was open for 1% of the time, Pallas kernels for 0%

profile of v4, /device:TPU:1, one launch (start us, length us, event | category | flops | bytes accessed | tf_op | source)
XLA Modules:
  0.0 371.5 jit_solution(8105256065415337472)
XLA Ops:
  7.2 0.0 all-gather.3.cloned.1.call-start
  7.2 0.7 convert_rsqrt_fusion
  8.0 0.3 copy-done
  8.2 2.3 fusion.6
  10.5 0.0 reduce-scatter.3.cloned.1.call-start
  10.6 76.6 %all-gather.3.cloned.1.call-done.panels_hbm = bf16[16384,512]{1,0:T(8,128)(2,1)} async-done(((bf16[512,512]{1,0:T(8,128)(2,1)}), bf16[16384,512]{1,0:T(8,128)(2,1)}) %all-gather.3.cloned.1.call-update) | async-done | bytes 16777232 | tf_op jit(solution)/shard_map/all_gather | solution.py:95
  87.1 20.3 %shard_map.103 = f32[2048,512]{1,0:T(8,128)} custom-call(s32[64]{0:T(128)} %rows_ref.3, s32[64]{0:T(128)} %cols_ref.3, bf16[64,128,128]{2,1,0:T(8,128)(2,1)} %tiles_ref.3, bf16[16384,512]{1,0:T(8,128)(2,1)} %all-gather.3.cloned.1.call-done.panels_hbm), custom_call_target="tpu_custom_call" | custom-call | tf_op jit(solution)/shard_map/pallas_call | solution.py:61
  107.5 0.0 all-gather.5.cloned.1.call-start
  107.5 45.9 %reduce-scatter.3.cloned.1.call-done = f32[512,512]{1,0:T(8,128)} async-done(((f32[2048,512]{1,0:T(8,128)}), f32[512,512]{1,0:T(8,128)}) %reduce-scatter.3.cloned.1.call-update) | async-done | bytes 1048592 | tf_op jit(solution)/shard_map/reduce_scatter | solution.py:99
  153.4 2.8 multiply_convert_fusion.1
  156.2 0.0 reduce-scatter.5.cloned.1.call-start
  156.3 73.0 %all-gather.5.cloned.1.call-done.panels_hbm = bf16[16384,512]{1,0:T(8,128)(2,1)} async-done(((bf16[512,512]{1,0:T(8,128)(2,1)}), bf16[16384,512]{1,0:T(8,128)(2,1)}) %all-gather.5.cloned.1.call-update) | async-done | bytes 16777232 | tf_op jit(solution)/shard_map/all_gather | solution.py:105
  229.2 20.3 %shard_map.104 = f32[2048,512]{1,0:T(8,128)} custom-call(s32[64]{0:T(128)} %rows_ref.3, s32[64]{0:T(128)} %cols_ref.3, bf16[64,128,128]{2,1,0:T(8,128)(2,1)} %tiles_ref.3, bf16[16384,512]{1,0:T(8,128)(2,1)} %all-gather.5.cloned.1.call-done.panels_hbm), custom_call_target="tpu_custom_call" | custom-call | tf_op jit(solution)/shard_map/pallas_call | solution.py:61
  249.6 8.2 %all_to_all.20 = f32[4,512,1]{1,2,0:T(1,128)S(1)} all-to-all(f32[4,512,1]{1,2,0:T(1,128)S(1)} %broadcast_in_dim.6), channel_id=1, replica_groups=mesh['rows'=32,'rep'=4] {'rep'}, dimensions={0} | all-to-all | bytes 16384 | tf_op jit(solution)/shard_map/all_to_all | solution.py:83
  257.8 0.2 broadcast_in_dim.7
  258.0 51.2 %all_to_all.21 = bf16[4,512,512]{2,1,0:T(8,128)(2,1)S(1)} all-to-all(bf16[4,512,512]{2,1,0:T(8,128)(2,1)S(1)} %broadcast_in_dim.7), channel_id=1, replica_groups=mesh['rows'=32,'rep'=4] {'rep'}, dimensions={0} | all-to-all | bytes 4194304 | tf_op jit(solution)/shard_map/all_to_all | solution.py:83
  309.2 1.5 fusion.3
  310.6 0.3 reshape.25
  310.9 26.8 %all_to_all.22 = f32[128,4,512]{2,1,0:T(4,128)S(1)} all-to-all(f32[128,4,512]{2,1,0:T(4,128)S(1)} %reshape.25), channel_id=1, replica_groups=mesh['rows'=32,'rep'=4] {'rows','rep'}, dimensions={0} | all-to-all | bytes 2097152 | tf_op jit(solution)/shard_map/all_to_all | solution.py:74
  337.8 0.2 reduce_sum.9
  338.0 0.1 broadcast_in_dim.8
  338.1 23.0 %all_to_all.23 = f32[128,4,512]{2,1,0:T(4,128)S(1)} all-to-all(f32[128,4,512]{2,1,0:T(4,128)S(1)} %broadcast_in_dim.8), channel_id=1, replica_groups=mesh['rows'=32,'rep'=4] {'rows','rep'}, dimensions={0} | all-to-all | bytes 2097152 | tf_op jit(solution)/shard_map/all_to_all | solution.py:77
  361.1 1.3 reshape.26
  362.5 2.5 convolution_convert_fusion
  (15 shorter events, 0.1 us)
Async XLA Ops:
  7.2 1.1 copy-start
  7.2 80.0 %all-gather.3.cloned.1.call-start = ((), (), s32[]{:S(2)}) async-start(), calls=%async_computation.6 | async-start | bytes 17301504 | tf_op jit(solution)/shard_map/all_gather | solution.py:95
  10.5 142.9 %reduce-scatter.3.cloned.1.call-start = ((), (), s32[]{:S(2)}) async-start(), calls=%async_computation.7 | async-start | bytes 5242880 | tf_op jit(solution)/shard_map/reduce_scatter | solution.py:99
  107.4 46.0 %copy-start.2 = (bf16[512,512]{1,0:T(8,128)(2,1)S(1)}, bf16[512,512]{1,0:T(8,128)(2,1)}, u32[]{:S(2)}) copy-start(bf16[512,512]{1,0:T(8,128)(2,1)} %param.15) | copy-start | bytes 1572868
  107.5 46.0 %copy-start.4 = (f32[512]{0:T(512)S(1)}, f32[512]{0:T(512)}, u32[]{:S(2)}) copy-start(f32[512]{0:T(512)} %param.10) | copy-start | bytes 6148
  107.5 121.8 %all-gather.5.cloned.1.call-start = ((), (), s32[]{:S(2)}) async-start(), calls=%async_computation.8 | async-start | bytes 17301504 | tf_op jit(solution)/shard_map/all_gather | solution.py:105
  156.2 206.2 %reduce-scatter.5.cloned.1.call-start = ((), (), s32[]{:S(2)}) async-start(), calls=%async_computation.9 | async-start | bytes 5242880 | tf_op jit(solution)/shard_map/reduce_scatter | solution.py:107
  249.5 8.3 %copy-start.3 = (bf16[512,512]{1,0:T(8,128)(2,1)S(1)}, bf16[512,512]{1,0:T(8,128)(2,1)}, u32[]{:S(2)}) copy-start(bf16[512,512]{1,0:T(8,128)(2,1)} %param.8) | copy-start | bytes 1572868
  249.6 59.6 %copy-start.1 = (f32[2048,512]{1,0:T(8,128)S(1)}, f32[2048,512]{1,0:T(8,128)}, u32[]{:S(2)}) copy-start(f32[2048,512]{1,0:T(8,128)} %shard_map.104) | copy-start | bytes 12582916
Sparse Core Ops, SparseCore 0:
  10.8 76.2 all-gather.2
  107.6 45.7 reduce-scatter.2
  156.4 72.8 all-gather.4
  249.7 68.2 reduce-scatter.4

commit v5 on v4

--- a/solution.py
+++ b/solution.py
@@ -95,6 +95,7 @@
     panels = lax.all_gather(scaled, "rows", axis=0, tiled=True)
     slab_features = gather_by_exchange(features, "rep")
     slab_scale = gather_by_exchange(row_scale, "rep")
+    panels, slab_features, slab_scale = lax.optimization_barrier((panels, slab_features, slab_scale))
     slab_part = aggregate_slots(panels, tile_row, tile_col, tile_value, rep_count * block_count)
     aggregate = lax.psum_scatter(slab_part, "rep", scatter_dimension=0, tiled=True) * row_scale
     pre_act = aggregate + out_bias

time: 373 us -> 328 us (0.88)
  waiting for transfers between devices: 195 us -> 166 us
  blocking collectives: 109 us -> 89.2 us
    all_gather x1, waiting for transfers between devices: 76.6 us -> 39.9 us  [shards(): panels = lax.all_gather(scaled, 'rows', axis=0, tiled=True)]
    all_to_all x2, blocking collectives: 59.4 us -> 35.5 us  [gather_by_exchange(): lax.all_to_all(copies, axis, 0, 0, tiled=True)]
    reduce_scatter x1, waiting for transfers between devices: 0.01 us -> 7.01 us  [shards(): lax.psum_scatter(back_part, 'rep', scatter_dimension=0, tiled=True)]
  transfers between devices with their start and end apart: 4 -> 4, of which waited for: 3 -> 4; matrix products, arithmetic and copies ran while one was open for 1% -> 3% of each run, Pallas kernels for 0% -> 0%
where the time goes in v5:
time: 328 us; the launch traced here: 327 us
  waiting for transfers between devices  166 us (51%)
  blocking collectives  89.2 us (27%)
  Pallas kernels  40.6 us (12%)
  between operations  13.8 us (4%)
  matrix products  9.26 us (3%)
  local copies, waits for them, and re-layouts  4.49 us (1%)
  other arithmetic  3.73 us (1%)
    all_gather x1, waiting for transfers between devices, shards(): grad_panels = lax.all_gather(scaled_grad, 'rows', axis=0, tiled=True)  73 us
    reduce_scatter x1, waiting for transfers between devices, shards(): lax.psum_scatter(slab_part, 'rep', scatter_dimension=0, tiled=True)  45.9 us
    pallas_call x2, Pallas kernels, aggregate_slots(): pl.pallas_call(_aggregate_kernel, grid_spec=grid_spec, out_shape=jax.Shap...  40.6 us
    all_gather x1, waiting for transfers between devices, shards(): panels = lax.all_gather(scaled, 'rows', axis=0, tiled=True)  39.9 us
    all_to_all x2, blocking collectives, gather_by_exchange(): lax.all_to_all(copies, axis, 0, 0, tiled=True)  35.5 us
    all_to_all x1, blocking collectives, all_reduce_by_exchange(): lax.all_to_all(value.reshape(count, rows // count, width), axes, 0, 0, ti...  27.6 us
    all_to_all x1, blocking collectives, all_reduce_by_exchange(): return lax.all_to_all(spread, axes, 0, 0, tiled=True).reshape(rows, width)  26.1 us
    reduce_scatter x1, waiting for transfers between devices, shards(): lax.psum_scatter(back_part, 'rep', scatter_dimension=0, tiled=True)  7.01 us
  transfers between devices with their start and end apart: 4, of which 4 were waited for; matrix products, arithmetic and copies ran while one was open for 3% of the time, Pallas kernels for 0%

profile of v5, /device:TPU:1, one launch (start us, length us, event | category | flops | bytes accessed | tf_op | source)
XLA Modules:
  0.0 327.0 jit_solution(4591282151460413469)
XLA Ops:
  7.2 0.7 convert_rsqrt_fusion
  8.0 0.3 copy-done
  8.2 2.3 fusion.3
  10.5 0.0 reduce-scatter.3.cloned.1.call-start
  10.6 9.0 %all_to_all.20 = f32[4,512,1]{1,2,0:T(1,128)S(1)} all-to-all(f32[4,512,1]{1,2,0:T(1,128)S(1)} %broadcast_in_dim.7), channel_id=1, replica_groups=mesh['rows'=32,'rep'=4] {'rep'}, dimensions={0} | all-to-all | bytes 16384 | tf_op jit(solution)/shard_map/all_to_all | solution.py:83
  19.6 1.2 broadcast_in_dim.6
  20.8 26.5 %all_to_all.21 = bf16[4,512,512]{2,1,0:T(8,128)(2,1)S(1)} all-to-all(bf16[4,512,512]{2,1,0:T(8,128)(2,1)S(1)} %broadcast_in_dim.6), channel_id=1, replica_groups=mesh['rows'=32,'rep'=4] {'rep'}, dimensions={0} | all-to-all | bytes 4194304 | tf_op jit(solution)/shard_map/all_to_all | solution.py:83
  47.3 39.9 %all-gather.3.cloned.1.call-done.panels_hbm = bf16[16384,512]{1,0:T(8,128)(2,1)} async-done(((bf16[512,512]{1,0:T(8,128)(2,1)}), bf16[16384,512]{1,0:T(8,128)(2,1)}) %all-gather.3.cloned.1.call-update) | async-done | bytes 16777232 | tf_op jit(solution)/shard_map/all_gather | solution.py:95
  87.1 20.3 %shard_map.103 = f32[2048,512]{1,0:T(8,128)} custom-call(s32[64]{0:T(128)} %rows_ref.3, s32[64]{0:T(128)} %cols_ref.3, bf16[64,128,128]{2,1,0:T(8,128)(2,1)} %tiles_ref.3, bf16[16384,512]{1,0:T(8,128)(2,1)} %all-gather.3.cloned.1.call-done.panels_hbm), custom_call_target="tpu_custom_call" | custom-call | tf_op jit(solution)/shard_map/pallas_call | solution.py:61
  107.5 0.0 all-gather.5.cloned.1.call-start
  107.5 45.9 %reduce-scatter.3.cloned.1.call-done = f32[512,512]{1,0:T(8,128)} async-done(((f32[2048,512]{1,0:T(8,128)}), f32[512,512]{1,0:T(8,128)}) %reduce-scatter.3.cloned.1.call-update) | async-done | bytes 1048592 | tf_op jit(solution)/shard_map/reduce_scatter | solution.py:100
  153.4 2.8 multiply_convert_fusion.1
  156.2 0.0 reduce-scatter.5.cloned.1.call-start
  156.3 73.0 %all-gather.5.cloned.1.call-done.panels_hbm = bf16[16384,512]{1,0:T(8,128)(2,1)} async-done(((bf16[512,512]{1,0:T(8,128)(2,1)}), bf16[16384,512]{1,0:T(8,128)(2,1)}) %all-gather.5.cloned.1.call-update) | async-done | bytes 16777232 | tf_op jit(solution)/shard_map/all_gather | solution.py:106
  229.2 20.3 %shard_map.104 = f32[2048,512]{1,0:T(8,128)} custom-call(s32[64]{0:T(128)} %rows_ref.3, s32[64]{0:T(128)} %cols_ref.3, bf16[64,128,128]{2,1,0:T(8,128)(2,1)} %tiles_ref.3, bf16[16384,512]{1,0:T(8,128)(2,1)} %all-gather.5.cloned.1.call-done.panels_hbm), custom_call_target="tpu_custom_call" | custom-call | tf_op jit(solution)/shard_map/pallas_call | solution.py:61
  249.6 4.5 %fusion = f32[512,512]{1,0:T(8,128)} fusion(bf16[2048,512]{1,0:T(8,128)(2,1)S(1)} %bitcast.7, f32[2048,512]{1,0:T(8,128)} %shard_map.104, f32[2048]{0:T(1024)S(1)} %bitcast.8), kind=kOutput, calls=%fused_computation | convolution fusion | flops 1074790400 | bytes 7348224 | tf_op jit(solution)/shard_map/dot_general | solution.py:113
  254.1 1.5 reshape.27
  255.6 27.6 %all_to_all.22 = f32[128,4,512]{2,1,0:T(4,128)S(1)} all-to-all(f32[128,4,512]{2,1,0:T(4,128)S(1)} %reshape.27), channel_id=1, replica_groups=mesh['rows'=32,'rep'=4] {'rows','rep'}, dimensions={0} | all-to-all | bytes 2097152 | tf_op jit(solution)/shard_map/all_to_all | solution.py:74
  283.2 0.2 reduce_sum.9
  283.4 0.1 broadcast_in_dim.8
  283.6 26.1 %all_to_all.23 = f32[128,4,512]{2,1,0:T(4,128)S(1)} all-to-all(f32[128,4,512]{2,1,0:T(4,128)S(1)} %broadcast_in_dim.8), channel_id=1, replica_groups=mesh['rows'=32,'rep'=4] {'rows','rep'}, dimensions={0} | all-to-all | bytes 2097152 | tf_op jit(solution)/shard_map/all_to_all | solution.py:77
  309.6 1.3 reshape.28
  311.0 7.0 %reduce-scatter.5.cloned.1.call-done = f32[512,512]{1,0:T(8,128)} async-done(((f32[2048,512]{1,0:T(8,128)}), f32[512,512]{1,0:T(8,128)}) %reduce-scatter.5.cloned.1.call-update) | async-done | bytes 1048592 | tf_op jit(solution)/shard_map/reduce_scatter | solution.py:108
  318.0 2.5 convolution_convert_fusion
  (11 shorter events, 0.1 us)
Async XLA Ops:
  7.2 1.1 copy-start
  7.2 80.0 %all-gather.3.cloned.1.call-start = ((), (), s32[]{:S(2)}) async-start(), calls=%async_computation.6 | async-start | bytes 17301504 | tf_op jit(solution)/shard_map/all_gather | solution.py:95
  10.5 142.9 %reduce-scatter.3.cloned.1.call-start = ((), (), s32[]{:S(2)}) async-start(), calls=%async_computation.7 | async-start | bytes 5242880 | tf_op jit(solution)/shard_map/reduce_scatter | solution.py:100
  107.4 46.0 %copy-start.1 = (bf16[512,512]{1,0:T(8,128)(2,1)S(1)}, bf16[512,512]{1,0:T(8,128)(2,1)}, u32[]{:S(2)}) copy-start(bf16[512,512]{1,0:T(8,128)(2,1)} %param.15) | copy-start | bytes 1572868
  107.5 46.0 %copy-start.2 = (f32[512]{0:T(512)S(1)}, f32[512]{0:T(512)}, u32[]{:S(2)}) copy-start(f32[512]{0:T(512)} %param.10) | copy-start | bytes 6148
  107.5 121.8 %all-gather.5.cloned.1.call-start = ((), (), s32[]{:S(2)}) async-start(), calls=%async_computation.8 | async-start | bytes 17301504 | tf_op jit(solution)/shard_map/all_gather | solution.py:106
  156.2 161.7 %reduce-scatter.5.cloned.1.call-start = ((), (), s32[]{:S(2)}) async-start(), calls=%async_computation.9 | async-start | bytes 5242880 | tf_op jit(solution)/shard_map/reduce_scatter | solution.py:108
Sparse Core Ops, SparseCore 0:
  10.8 76.2 all-gather.2
  107.6 45.7 reduce-scatter.2
  156.4 72.8 all-gather.4
  249.7 68.2 reduce-scatter.4

commit v6 on v5

--- a/solution.py
+++ b/solution.py
@@ -6,7 +6,7 @@
 from jax.sharding import PartitionSpec as P
 
 
-PANEL_BUFFERS = 4
+PANEL_BUFFERS = 8
 
 
 def _aggregate_kernel(rows_ref, cols_ref, tiles_ref, panels_hbm, out_ref, buffers, sems):
@@ -39,7 +39,7 @@
 
         return carry
 
-    lax.fori_loop(0, slot_count, step, 0)
+    lax.fori_loop(0, slot_count, step, 0, unroll=2)
 
 
 def aggregate_slots(panels, group_rows, group_cols, tiles, out_blocks):

time: 328 us -> 320 us (0.976)
  Pallas kernels: 40.6 us -> 32.7 us
    pallas_call x2, Pallas kernels: 40.6 us -> 32.7 us  [aggregate_slots(): pl.pallas_call(_aggregate_kernel, grid_spec=grid_spec, out_shape=jax.Shap...]
where the time goes in v6:
time: 320 us; the launch traced here: 319 us
  waiting for transfers between devices  166 us (52%)
  blocking collectives  89.1 us (28%)
  Pallas kernels  32.7 us (10%)
  between operations  13.8 us (4%)
  matrix products  9.26 us (3%)
  local copies, waits for them, and re-layouts  4.49 us (1%)
  other arithmetic  3.73 us (1%)
    all_gather x1, waiting for transfers between devices, shards(): grad_panels = lax.all_gather(scaled_grad, 'rows', axis=0, tiled=True)  73 us
    reduce_scatter x1, waiting for transfers between devices, shards(): lax.psum_scatter(slab_part, 'rep', scatter_dimension=0, tiled=True)  45.9 us
    all_gather x1, waiting for transfers between devices, shards(): panels = lax.all_gather(scaled, 'rows', axis=0, tiled=True)  39.9 us
    all_to_all x2, blocking collectives, gather_by_exchange(): lax.all_to_all(copies, axis, 0, 0, tiled=True)  35.5 us
    pallas_call x2, Pallas kernels, aggregate_slots(): pl.pallas_call(_aggregate_kernel, grid_spec=grid_spec, out_shape=jax.Shap...  32.7 us
    all_to_all x1, blocking collectives, all_reduce_by_exchange(): lax.all_to_all(value.reshape(count, rows // count, width), axes, 0, 0, ti...  27.6 us
    all_to_all x1, blocking collectives, all_reduce_by_exchange(): return lax.all_to_all(spread, axes, 0, 0, tiled=True).reshape(rows, width)  26.1 us
    reduce_scatter x1, waiting for transfers between devices, shards(): lax.psum_scatter(back_part, 'rep', scatter_dimension=0, tiled=True)  6.99 us
  transfers between devices with their start and end apart: 4, of which 4 were waited for; matrix products, arithmetic and copies ran while one was open for 3% of the time, Pallas kernels for 0%

profile of v6, /device:TPU:1, one launch (start us, length us, event | category | flops | bytes accessed | tf_op | source)
XLA Modules:
  0.0 319.1 jit_solution(12973497194671113682)
XLA Ops:
  7.2 0.7 convert_rsqrt_fusion
  8.0 0.3 copy-done
  8.2 2.3 fusion.3
  10.5 0.0 reduce-scatter.3.cloned.1.call-start
  10.6 9.0 %all_to_all.20 = f32[4,512,1]{1,2,0:T(1,128)S(1)} all-to-all(f32[4,512,1]{1,2,0:T(1,128)S(1)} %broadcast_in_dim.7), channel_id=1, replica_groups=mesh['rows'=32,'rep'=4] {'rep'}, dimensions={0} | all-to-all | bytes 16384 | tf_op jit(solution)/shard_map/all_to_all | solution.py:83
  19.6 1.2 broadcast_in_dim.6
  20.8 26.5 %all_to_all.21 = bf16[4,512,512]{2,1,0:T(8,128)(2,1)S(1)} all-to-all(bf16[4,512,512]{2,1,0:T(8,128)(2,1)S(1)} %broadcast_in_dim.6), channel_id=1, replica_groups=mesh['rows'=32,'rep'=4] {'rep'}, dimensions={0} | all-to-all | bytes 4194304 | tf_op jit(solution)/shard_map/all_to_all | solution.py:83
  47.3 39.9 %all-gather.3.cloned.1.call-done.panels_hbm = bf16[16384,512]{1,0:T(8,128)(2,1)} async-done(((bf16[512,512]{1,0:T(8,128)(2,1)}), bf16[16384,512]{1,0:T(8,128)(2,1)}) %all-gather.3.cloned.1.call-update) | async-done | bytes 16777232 | tf_op jit(solution)/shard_map/all_gather | solution.py:95
  87.1 16.3 %shard_map.103 = f32[2048,512]{1,0:T(8,128)} custom-call(s32[64]{0:T(128)} %rows_ref.3, s32[64]{0:T(128)} %cols_ref.3, bf16[64,128,128]{2,1,0:T(8,128)(2,1)} %tiles_ref.3, bf16[16384,512]{1,0:T(8,128)(2,1)} %all-gather.3.cloned.1.call-done.panels_hbm), custom_call_target="tpu_custom_call" | custom-call | tf_op jit(solution)/shard_map/pallas_call | solution.py:61
  103.5 0.0 all-gather.5.cloned.1.call-start
  103.6 45.9 %reduce-scatter.3.cloned.1.call-done = f32[512,512]{1,0:T(8,128)} async-done(((f32[2048,512]{1,0:T(8,128)}), f32[512,512]{1,0:T(8,128)}) %reduce-scatter.3.cloned.1.call-update) | async-done | bytes 1048592 | tf_op jit(solution)/shard_map/reduce_scatter | solution.py:100
  149.5 2.8 multiply_convert_fusion.1
  152.3 0.0 reduce-scatter.5.cloned.1.call-start
  152.4 73.0 %all-gather.5.cloned.1.call-done.panels_hbm = bf16[16384,512]{1,0:T(8,128)(2,1)} async-done(((bf16[512,512]{1,0:T(8,128)(2,1)}), bf16[16384,512]{1,0:T(8,128)(2,1)}) %all-gather.5.cloned.1.call-update) | async-done | bytes 16777232 | tf_op jit(solution)/shard_map/all_gather | solution.py:106
  225.3 16.4 %shard_map.104 = f32[2048,512]{1,0:T(8,128)} custom-call(s32[64]{0:T(128)} %rows_ref.3, s32[64]{0:T(128)} %cols_ref.3, bf16[64,128,128]{2,1,0:T(8,128)(2,1)} %tiles_ref.3, bf16[16384,512]{1,0:T(8,128)(2,1)} %all-gather.5.cloned.1.call-done.panels_hbm), custom_call_target="tpu_custom_call" | custom-call | tf_op jit(solution)/shard_map/pallas_call | solution.py:61
  241.7 4.5 %fusion = f32[512,512]{1,0:T(8,128)} fusion(bf16[2048,512]{1,0:T(8,128)(2,1)S(1)} %bitcast.7, f32[2048,512]{1,0:T(8,128)} %shard_map.104, f32[2048]{0:T(1024)S(1)} %bitcast.8), kind=kOutput, calls=%fused_computation | convolution fusion | flops 1074790400 | bytes 7348224 | tf_op jit(solution)/shard_map/dot_general | solution.py:113
  246.2 1.5 reshape.27
  247.7 27.6 %all_to_all.22 = f32[128,4,512]{2,1,0:T(4,128)S(1)} all-to-all(f32[128,4,512]{2,1,0:T(4,128)S(1)} %reshape.27), channel_id=1, replica_groups=mesh['rows'=32,'rep'=4] {'rows','rep'}, dimensions={0} | all-to-all | bytes 2097152 | tf_op jit(solution)/shard_map/all_to_all | solution.py:74
  275.3 0.2 reduce_sum.9
  275.5 0.1 broadcast_in_dim.8
  275.7 26.1 %all_to_all.23 = f32[128,4,512]{2,1,0:T(4,128)S(1)} all-to-all(f32[128,4,512]{2,1,0:T(4,128)S(1)} %broadcast_in_dim.8), channel_id=1, replica_groups=mesh['rows'=32,'rep'=4] {'rows','rep'}, dimensions={0} | all-to-all | bytes 2097152 | tf_op jit(solution)/shard_map/all_to_all | solution.py:77
  301.8 1.3 reshape.28
  303.1 7.0 %reduce-scatter.5.cloned.1.call-done = f32[512,512]{1,0:T(8,128)} async-done(((f32[2048,512]{1,0:T(8,128)}), f32[512,512]{1,0:T(8,128)}) %reduce-scatter.5.cloned.1.call-update) | async-done | bytes 1048592 | tf_op jit(solution)/shard_map/reduce_scatter | solution.py:108
  310.1 2.5 convolution_convert_fusion
  (11 shorter events, 0.1 us)
Async XLA Ops:
  7.2 1.1 copy-start
  7.2 80.0 %all-gather.3.cloned.1.call-start = ((), (), s32[]{:S(2)}) async-start(), calls=%async_computation.6 | async-start | bytes 17301504 | tf_op jit(solution)/shard_map/all_gather | solution.py:95
  10.5 139.0 %reduce-scatter.3.cloned.1.call-start = ((), (), s32[]{:S(2)}) async-start(), calls=%async_computation.7 | async-start | bytes 5242880 | tf_op jit(solution)/shard_map/reduce_scatter | solution.py:100
  103.5 46.0 %copy-start.1 = (bf16[512,512]{1,0:T(8,128)(2,1)S(1)}, bf16[512,512]{1,0:T(8,128)(2,1)}, u32[]{:S(2)}) copy-start(bf16[512,512]{1,0:T(8,128)(2,1)} %param.15) | copy-start | bytes 1572868
  103.5 46.0 %copy-start.2 = (f32[512]{0:T(512)S(1)}, f32[512]{0:T(512)}, u32[]{:S(2)}) copy-start(f32[512]{0:T(512)} %param.10) | copy-start | bytes 6148
  103.5 121.8 %all-gather.5.cloned.1.call-start = ((), (), s32[]{:S(2)}) async-start(), calls=%async_computation.8 | async-start | bytes 17301504 | tf_op jit(solution)/shard_map/all_gather | solution.py:106
  152.3 157.8 %reduce-scatter.5.cloned.1.call-start = ((), (), s32[]{:S(2)}) async-start(), calls=%async_computation.9 | async-start | bytes 5242880 | tf_op jit(solution)/shard_map/reduce_scatter | solution.py:108
Sparse Core Ops, SparseCore 0:
  10.8 76.2 all-gather.2
  103.6 45.8 reduce-scatter.2
  152.4 72.8 all-gather.4
  241.8 68.1 reduce-scatter.4

commit v7 on v6

--- a/solution.py
+++ b/solution.py
@@ -105,8 +105,8 @@
     scaled_grad = (grad_pre * row_scale).astype(jnp.bfloat16)
     grad_panels = lax.all_gather(scaled_grad, "rows", axis=0, tiled=True)
     back_part = aggregate_slots(grad_panels, tile_row, tile_col, tile_value, rep_count * block_count)
-    back_total = lax.psum_scatter(back_part, "rep", scatter_dimension=0, tiled=True)
-    back_sum = (back_total * row_scale).astype(jnp.bfloat16)
+    back_total = lax.psum_scatter(back_part.astype(jnp.bfloat16), "rep", scatter_dimension=0, tiled=True)
+    back_sum = (back_total.astype(jnp.float32) * row_scale).astype(jnp.bfloat16)
     grad_input = lax.dot_general(
         back_sum, weight, (((1,), (1,)), ((), ())), preferred_element_type=jnp.float32
     ).astype(jnp.bfloat16)

time: 320 us -> 315 us (0.984)
  waiting for transfers between devices: 166 us -> 159 us
  other arithmetic: 3.73 us -> 7.55 us
    reduce_scatter x1, waiting for transfers between devices: 6.99 us -> 0.01 us  [shards(): lax.psum_scatter(back_part.astype(jnp.bfloat16), 'rep', scatter_dimension...]
    convert_element_type x0 -> x1, other arithmetic: none -> 3.8 us  [shards(): back_part.astype(jnp.bfloat16)]
  transfers between devices with their start and end apart: 4 -> 4, of which waited for: 4 -> 3; matrix products, arithmetic and copies ran while one was open for 3% -> 3% of each run, Pallas kernels for 0% -> 0%
where the time goes in v7:
time: 315 us
  waiting for transfers between devices  159 us (50%)
  blocking collectives  88 us (28%)
  Pallas kernels  32.6 us (10%)
  between operations  13.8 us (4%)
  matrix products  9.18 us (3%)
  other arithmetic  7.55 us (2%)
  local copies, waits for them, and re-layouts  4.49 us (1%)
    all_gather x1, waiting for transfers between devices, shards(): grad_panels = lax.all_gather(scaled_grad, 'rows', axis=0, tiled=True)  73 us
    reduce_scatter x1, waiting for transfers between devices, shards(): lax.psum_scatter(slab_part, 'rep', scatter_dimension=0, tiled=True)  45.9 us
    all_gather x1, waiting for transfers between devices, shards(): panels = lax.all_gather(scaled, 'rows', axis=0, tiled=True)  39.9 us
    all_to_all x2, blocking collectives, gather_by_exchange(): lax.all_to_all(copies, axis, 0, 0, tiled=True)  35.5 us
    pallas_call x2, Pallas kernels, aggregate_slots(): pl.pallas_call(_aggregate_kernel, grid_spec=grid_spec, out_shape=jax.Shap...  32.6 us
    all_to_all x1, blocking collectives, all_reduce_by_exchange(): lax.all_to_all(value.reshape(count, rows // count, width), axes, 0, 0, ti...  27.7 us
    all_to_all x1, blocking collectives, all_reduce_by_exchange(): return lax.all_to_all(spread, axes, 0, 0, tiled=True).reshape(rows, width)  24.8 us
  transfers between devices with their start and end apart: 4, of which 3 were waited for; matrix products, arithmetic and copies ran while one was open for 3% of the time, Pallas kernels for 0%

profile of v7, /device:TPU:1, one launch (start us, length us, event | category | flops | bytes accessed | tf_op | source)
XLA Modules:
  0.0 314.7 jit_solution(3807405491303888617)
XLA Ops:
  7.2 0.7 convert_rsqrt_fusion
  8.0 0.3 copy-done
  8.2 2.3 fusion.3
  10.5 0.0 reduce-scatter.3.cloned.1.call-start
  10.6 9.0 %all_to_all.20 = f32[4,512,1]{1,2,0:T(1,128)S(1)} all-to-all(f32[4,512,1]{1,2,0:T(1,128)S(1)} %broadcast_in_dim.7), channel_id=1, replica_groups=mesh['rows'=32,'rep'=4] {'rep'}, dimensions={0} | all-to-all | bytes 16384 | tf_op jit(solution)/shard_map/all_to_all | solution.py:83
  19.6 1.2 broadcast_in_dim.6
  20.8 26.5 %all_to_all.21 = bf16[4,512,512]{2,1,0:T(8,128)(2,1)S(1)} all-to-all(bf16[4,512,512]{2,1,0:T(8,128)(2,1)S(1)} %broadcast_in_dim.6), channel_id=1, replica_groups=mesh['rows'=32,'rep'=4] {'rep'}, dimensions={0} | all-to-all | bytes 4194304 | tf_op jit(solution)/shard_map/all_to_all | solution.py:83
  47.3 39.9 %all-gather.3.cloned.1.call-done.panels_hbm = bf16[16384,512]{1,0:T(8,128)(2,1)} async-done(((bf16[512,512]{1,0:T(8,128)(2,1)}), bf16[16384,512]{1,0:T(8,128)(2,1)}) %all-gather.3.cloned.1.call-update) | async-done | bytes 16777232 | tf_op jit(solution)/shard_map/all_gather | solution.py:95
  87.1 16.3 %shard_map.103 = f32[2048,512]{1,0:T(8,128)} custom-call(s32[64]{0:T(128)} %rows_ref.3, s32[64]{0:T(128)} %cols_ref.3, bf16[64,128,128]{2,1,0:T(8,128)(2,1)} %tiles_ref.3, bf16[16384,512]{1,0:T(8,128)(2,1)} %all-gather.3.cloned.1.call-done.panels_hbm), custom_call_target="tpu_custom_call" | custom-call | tf_op jit(solution)/shard_map/pallas_call | solution.py:61
  103.5 0.0 all-gather.5.cloned.1.call-start
  103.6 45.9 %reduce-scatter.3.cloned.1.call-done = f32[512,512]{1,0:T(8,128)} async-done(((f32[2048,512]{1,0:T(8,128)}), f32[512,512]{1,0:T(8,128)}) %reduce-scatter.3.cloned.1.call-update) | async-done | bytes 1048592 | tf_op jit(solution)/shard_map/reduce_scatter | solution.py:100
  149.5 2.8 multiply_convert_fusion.1
  152.3 0.0 reduce-scatter.5.cloned.1.call-start
  152.4 73.0 %all-gather.5.cloned.1.call-done.panels_hbm = bf16[16384,512]{1,0:T(8,128)(2,1)} async-done(((bf16[512,512]{1,0:T(8,128)(2,1)}), bf16[16384,512]{1,0:T(8,128)(2,1)}) %all-gather.5.cloned.1.call-update) | async-done | bytes 16777232 | tf_op jit(solution)/shard_map/all_gather | solution.py:106
  225.3 16.3 %shard_map.104 = f32[2048,512]{1,0:T(8,128)} custom-call(s32[64]{0:T(128)} %rows_ref.3, s32[64]{0:T(128)} %cols_ref.3, bf16[64,128,128]{2,1,0:T(8,128)(2,1)} %tiles_ref.3, bf16[16384,512]{1,0:T(8,128)(2,1)} %all-gather.5.cloned.1.call-done.panels_hbm), custom_call_target="tpu_custom_call" | custom-call | tf_op jit(solution)/shard_map/pallas_call | solution.py:61
  241.7 3.8 %convert_element_type.32 = bf16[2048,512]{1,0:T(8,128)(2,1)} convert(f32[2048,512]{1,0:T(8,128)} %shard_map.104) | non-fusion elementwise | flops 1048576 | bytes 6291456 | tf_op jit(solution)/shard_map/convert_element_type | solution.py:108
  245.5 4.6 %fusion = f32[512,512]{1,0:T(8,128)} fusion(bf16[2048,512]{1,0:T(8,128)(2,1)S(1)} %bitcast.7, f32[2048,512]{1,0:T(8,128)} %shard_map.104, f32[2048]{0:T(1024)S(1)} %bitcast.8), kind=kOutput, calls=%fused_computation | convolution fusion | flops 1074790400 | bytes 7348224 | tf_op jit(solution)/shard_map/dot_general | solution.py:113
  250.1 1.5 reshape.27
  251.6 27.7 %all_to_all.22 = f32[128,4,512]{2,1,0:T(4,128)S(1)} all-to-all(f32[128,4,512]{2,1,0:T(4,128)S(1)} %reshape.27), channel_id=1, replica_groups=mesh['rows'=32,'rep'=4] {'rows','rep'}, dimensions={0} | all-to-all | bytes 2097152 | tf_op jit(solution)/shard_map/all_to_all | solution.py:74
  279.3 0.2 reduce_sum.9
  279.5 0.1 broadcast_in_dim.8
  279.6 24.8 %all_to_all.23 = f32[128,4,512]{2,1,0:T(4,128)S(1)} all-to-all(f32[128,4,512]{2,1,0:T(4,128)S(1)} %broadcast_in_dim.8), channel_id=1, replica_groups=mesh['rows'=32,'rep'=4] {'rows','rep'}, dimensions={0} | all-to-all | bytes 2097152 | tf_op jit(solution)/shard_map/all_to_all | solution.py:77
  304.5 1.3 reshape.28
  305.8 2.3 convolution_convert_fusion
  (12 shorter events, 0.1 us)
Async XLA Ops:
  7.2 1.1 copy-start
  7.2 80.0 %all-gather.3.cloned.1.call-start = ((), (), s32[]{:S(2)}) async-start(), calls=%async_computation.6 | async-start | bytes 17301504 | tf_op jit(solution)/shard_map/all_gather | solution.py:95
  10.5 139.0 %reduce-scatter.3.cloned.1.call-start = ((), (), s32[]{:S(2)}) async-start(), calls=%async_computation.7 | async-start | bytes 5242880 | tf_op jit(solution)/shard_map/reduce_scatter | solution.py:100
  103.5 46.0 %copy-start.1 = (bf16[512,512]{1,0:T(8,128)(2,1)S(1)}, bf16[512,512]{1,0:T(8,128)(2,1)}, u32[]{:S(2)}) copy-start(bf16[512,512]{1,0:T(8,128)(2,1)} %param.15) | copy-start | bytes 1572868
  103.5 46.0 %copy-start.2 = (f32[512]{0:T(512)S(1)}, f32[512]{0:T(512)}, u32[]{:S(2)}) copy-start(f32[512]{0:T(512)} %param.10) | copy-start | bytes 6148
  103.5 121.8 %all-gather.5.cloned.1.call-start = ((), (), s32[]{:S(2)}) async-start(), calls=%async_computation.8 | async-start | bytes 17301504 | tf_op jit(solution)/shard_map/all_gather | solution.py:106
  152.3 153.5 %reduce-scatter.5.cloned.1.call-start = ((), (), s32[]{:S(2)}) async-start(), calls=%async_computation.9 | async-start | bytes 2621440 | tf_op jit(solution)/shard_map/reduce_scatter | solution.py:108
Sparse Core Ops, SparseCore 0:
  10.8 76.2 all-gather.2
  103.6 45.8 reduce-scatter.2
  152.4 72.8 all-gather.4
  245.6 39.9 reduce-scatter.4

commit v8 on v6

--- a/solution.py
+++ b/solution.py
@@ -6,7 +6,7 @@
 from jax.sharding import PartitionSpec as P
 
 
-PANEL_BUFFERS = 8
+PANEL_BUFFERS = 16
 
 
 def _aggregate_kernel(rows_ref, cols_ref, tiles_ref, panels_hbm, out_ref, buffers, sems):
@@ -39,7 +39,7 @@
 
         return carry
 
-    lax.fori_loop(0, slot_count, step, 0, unroll=2)
+    lax.fori_loop(0, slot_count, step, 0, unroll=4)
 
 
 def aggregate_slots(panels, group_rows, group_cols, tiles, out_blocks):

time: 320 us -> 320 us (level)
  no operation moved by 1% of the time
where the time goes in v8:
time: 320 us; the launch traced here: 319 us
  waiting for transfers between devices  166 us (52%)
  blocking collectives  89.2 us (28%)
  Pallas kernels  32.8 us (10%)
  between operations  13.8 us (4%)
  matrix products  9.26 us (3%)
  local copies, waits for them, and re-layouts  4.49 us (1%)
  other arithmetic  3.73 us (1%)
    all_gather x1, waiting for transfers between devices, shards(): grad_panels = lax.all_gather(scaled_grad, 'rows', axis=0, tiled=True)  73 us
    reduce_scatter x1, waiting for transfers between devices, shards(): lax.psum_scatter(slab_part, 'rep', scatter_dimension=0, tiled=True)  45.9 us
    all_gather x1, waiting for transfers between devices, shards(): panels = lax.all_gather(scaled, 'rows', axis=0, tiled=True)  39.9 us
    all_to_all x2, blocking collectives, gather_by_exchange(): lax.all_to_all(copies, axis, 0, 0, tiled=True)  35.5 us
    pallas_call x2, Pallas kernels, aggregate_slots(): pl.pallas_call(_aggregate_kernel, grid_spec=grid_spec, out_shape=jax.Shap...  32.8 us
    all_to_all x1, blocking collectives, all_reduce_by_exchange(): lax.all_to_all(value.reshape(count, rows // count, width), axes, 0, 0, ti...  27.6 us
    all_to_all x1, blocking collectives, all_reduce_by_exchange(): return lax.all_to_all(spread, axes, 0, 0, tiled=True).reshape(rows, width)  26.1 us
    reduce_scatter x1, waiting for transfers between devices, shards(): lax.psum_scatter(back_part, 'rep', scatter_dimension=0, tiled=True)  7.01 us
  transfers between devices with their start and end apart: 4, of which 4 were waited for; matrix products, arithmetic and copies ran while one was open for 3% of the time, Pallas kernels for 0%

profile of v8, /device:TPU:1, one launch (start us, length us, event | category | flops | bytes accessed | tf_op | source)
XLA Modules:
  0.0 319.3 jit_solution(10398977970689333559)
XLA Ops:
  7.2 0.7 convert_rsqrt_fusion
  8.0 0.3 copy-done
  8.2 2.3 fusion.3
  10.5 0.0 reduce-scatter.3.cloned.1.call-start
  10.6 9.0 %all_to_all.20 = f32[4,512,1]{1,2,0:T(1,128)S(1)} all-to-all(f32[4,512,1]{1,2,0:T(1,128)S(1)} %broadcast_in_dim.7), channel_id=1, replica_groups=mesh['rows'=32,'rep'=4] {'rep'}, dimensions={0} | all-to-all | bytes 16384 | tf_op jit(solution)/shard_map/all_to_all | solution.py:83
  19.6 1.2 broadcast_in_dim.6
  20.8 26.5 %all_to_all.21 = bf16[4,512,512]{2,1,0:T(8,128)(2,1)S(1)} all-to-all(bf16[4,512,512]{2,1,0:T(8,128)(2,1)S(1)} %broadcast_in_dim.6), channel_id=1, replica_groups=mesh['rows'=32,'rep'=4] {'rep'}, dimensions={0} | all-to-all | bytes 4194304 | tf_op jit(solution)/shard_map/all_to_all | solution.py:83
  47.3 39.9 %all-gather.3.cloned.1.call-done.panels_hbm = bf16[16384,512]{1,0:T(8,128)(2,1)} async-done(((bf16[512,512]{1,0:T(8,128)(2,1)}), bf16[16384,512]{1,0:T(8,128)(2,1)}) %all-gather.3.cloned.1.call-update) | async-done | bytes 16777232 | tf_op jit(solution)/shard_map/all_gather | solution.py:95
  87.1 16.4 %shard_map.103 = f32[2048,512]{1,0:T(8,128)} custom-call(s32[64]{0:T(128)} %rows_ref.3, s32[64]{0:T(128)} %cols_ref.3, bf16[64,128,128]{2,1,0:T(8,128)(2,1)} %tiles_ref.3, bf16[16384,512]{1,0:T(8,128)(2,1)} %all-gather.3.cloned.1.call-done.panels_hbm), custom_call_target="tpu_custom_call" | custom-call | tf_op jit(solution)/shard_map/pallas_call | solution.py:61
  103.6 0.0 all-gather.5.cloned.1.call-start
  103.7 45.9 %reduce-scatter.3.cloned.1.call-done = f32[512,512]{1,0:T(8,128)} async-done(((f32[2048,512]{1,0:T(8,128)}), f32[512,512]{1,0:T(8,128)}) %reduce-scatter.3.cloned.1.call-update) | async-done | bytes 1048592 | tf_op jit(solution)/shard_map/reduce_scatter | solution.py:100
  149.5 2.8 multiply_convert_fusion.1
  152.4 0.0 reduce-scatter.5.cloned.1.call-start
  152.4 73.0 %all-gather.5.cloned.1.call-done.panels_hbm = bf16[16384,512]{1,0:T(8,128)(2,1)} async-done(((bf16[512,512]{1,0:T(8,128)(2,1)}), bf16[16384,512]{1,0:T(8,128)(2,1)}) %all-gather.5.cloned.1.call-update) | async-done | bytes 16777232 | tf_op jit(solution)/shard_map/all_gather | solution.py:106
  225.4 16.4 %shard_map.104 = f32[2048,512]{1,0:T(8,128)} custom-call(s32[64]{0:T(128)} %rows_ref.3, s32[64]{0:T(128)} %cols_ref.3, bf16[64,128,128]{2,1,0:T(8,128)(2,1)} %tiles_ref.3, bf16[16384,512]{1,0:T(8,128)(2,1)} %all-gather.5.cloned.1.call-done.panels_hbm), custom_call_target="tpu_custom_call" | custom-call | tf_op jit(solution)/shard_map/pallas_call | solution.py:61
  241.8 4.5 %fusion = f32[512,512]{1,0:T(8,128)} fusion(bf16[2048,512]{1,0:T(8,128)(2,1)S(1)} %bitcast.7, f32[2048,512]{1,0:T(8,128)} %shard_map.104, f32[2048]{0:T(1024)S(1)} %bitcast.8), kind=kOutput, calls=%fused_computation | convolution fusion | flops 1074790400 | bytes 7348224 | tf_op jit(solution)/shard_map/dot_general | solution.py:113
  246.3 1.5 reshape.27
  247.8 27.6 %all_to_all.22 = f32[128,4,512]{2,1,0:T(4,128)S(1)} all-to-all(f32[128,4,512]{2,1,0:T(4,128)S(1)} %reshape.27), channel_id=1, replica_groups=mesh['rows'=32,'rep'=4] {'rows','rep'}, dimensions={0} | all-to-all | bytes 2097152 | tf_op jit(solution)/shard_map/all_to_all | solution.py:74
  275.5 0.2 reduce_sum.9
  275.7 0.1 broadcast_in_dim.8
  275.8 26.1 %all_to_all.23 = f32[128,4,512]{2,1,0:T(4,128)S(1)} all-to-all(f32[128,4,512]{2,1,0:T(4,128)S(1)} %broadcast_in_dim.8), channel_id=1, replica_groups=mesh['rows'=32,'rep'=4] {'rows','rep'}, dimensions={0} | all-to-all | bytes 2097152 | tf_op jit(solution)/shard_map/all_to_all | solution.py:77
  301.9 1.3 reshape.28
  303.2 7.0 %reduce-scatter.5.cloned.1.call-done = f32[512,512]{1,0:T(8,128)} async-done(((f32[2048,512]{1,0:T(8,128)}), f32[512,512]{1,0:T(8,128)}) %reduce-scatter.5.cloned.1.call-update) | async-done | bytes 1048592 | tf_op jit(solution)/shard_map/reduce_scatter | solution.py:108
  310.2 2.5 convolution_convert_fusion
  (11 shorter events, 0.1 us)
Async XLA Ops:
  7.2 1.1 copy-start
  7.2 80.0 %all-gather.3.cloned.1.call-start = ((), (), s32[]{:S(2)}) async-start(), calls=%async_computation.6 | async-start | bytes 17301504 | tf_op jit(solution)/shard_map/all_gather | solution.py:95
  10.5 139.0 %reduce-scatter.3.cloned.1.call-start = ((), (), s32[]{:S(2)}) async-start(), calls=%async_computation.7 | async-start | bytes 5242880 | tf_op jit(solution)/shard_map/reduce_scatter | solution.py:100
  103.6 46.0 %copy-start.1 = (bf16[512,512]{1,0:T(8,128)(2,1)S(1)}, bf16[512,512]{1,0:T(8,128)(2,1)}, u32[]{:S(2)}) copy-start(bf16[512,512]{1,0:T(8,128)(2,1)} %param.15) | copy-start | bytes 1572868
  103.6 46.0 %copy-start.2 = (f32[512]{0:T(512)S(1)}, f32[512]{0:T(512)}, u32[]{:S(2)}) copy-start(f32[512]{0:T(512)} %param.10) | copy-start | bytes 6148
  103.6 121.8 %all-gather.5.cloned.1.call-start = ((), (), s32[]{:S(2)}) async-start(), calls=%async_computation.8 | async-start | bytes 17301504 | tf_op jit(solution)/shard_map/all_gather | solution.py:106
  152.4 157.9 %reduce-scatter.5.cloned.1.call-start = ((), (), s32[]{:S(2)}) async-start(), calls=%async_computation.9 | async-start | bytes 5242880 | tf_op jit(solution)/shard_map/reduce_scatter | solution.py:108
Sparse Core Ops, SparseCore 0:
  10.8 76.2 all-gather.2
  103.7 45.7 reduce-scatter.2
  152.5 72.8 all-gather.4
  242.0 68.2 reduce-scatter.4

commit v9 on v6

--- a/solution.py
+++ b/solution.py
@@ -9,8 +9,8 @@
 PANEL_BUFFERS = 8
 
 
-def _aggregate_kernel(rows_ref, cols_ref, tiles_ref, panels_hbm, out_ref, buffers, sems):
-    slot_count, tile_size, _ = tiles_ref.shape
+def _aggregate_kernel(rows_ref, cols_ref, tiles_hbm, panels_hbm, out_ref, buffers, tile_buffers, sems, tile_sems):
+    slot_count, tile_size, _ = tiles_hbm.shape
     panel_blocks = panels_hbm.shape[0] // tile_size
     out_blocks = out_ref.shape[0] // tile_size
 
@@ -21,20 +21,26 @@
             panels_hbm.at[pl.ds(start, tile_size), :], buffers.at[buffer], sems.at[buffer]
         )
 
+    def tile_copy(s, buffer):
+        return pltpu.make_async_copy(tiles_hbm.at[s], tile_buffers.at[buffer], tile_sems.at[buffer])
+
     for buffer in range(PANEL_BUFFERS):
+        tile_copy(buffer, buffer).start()
         panel_copy(buffer, buffer).start()
     out_ref[...] = jnp.zeros_like(out_ref)
 
     def step(s, carry):
         buffer = s % PANEL_BUFFERS
+        tile_copy(s, buffer).wait()
         panel_copy(s, buffer).wait()
         row = jnp.clip(rows_ref[s], 0, out_blocks - 1)
         start = pl.multiple_of(row * tile_size, tile_size)
-        product = jnp.dot(tiles_ref[s], buffers[buffer], preferred_element_type=jnp.float32)
+        product = jnp.dot(tile_buffers[buffer], buffers[buffer], preferred_element_type=jnp.float32)
         out_ref[pl.ds(start, tile_size), :] += product
 
         @pl.when(s + PANEL_BUFFERS < slot_count)
         def _():
+            tile_copy(s + PANEL_BUFFERS, buffer).start()
             panel_copy(s + PANEL_BUFFERS, buffer).start()
 
         return carry
@@ -49,12 +55,14 @@
         num_scalar_prefetch=2,
         grid=(1,),
         in_specs=[
-            pl.BlockSpec((slot_count, tile_size, tile_size), lambda i, rows, cols: (0, 0, 0)),
+            pl.BlockSpec(memory_space=pl.ANY),
             pl.BlockSpec(memory_space=pl.ANY),
         ],
         out_specs=pl.BlockSpec((out_blocks * tile_size, feat_width), lambda i, rows, cols: (0, 0)),
         scratch_shapes=[
             pltpu.VMEM((PANEL_BUFFERS, tile_size, feat_width), panels.dtype),
+            pltpu.VMEM((PANEL_BUFFERS, tile_size, tile_size), tiles.dtype),
+            pltpu.SemaphoreType.DMA((PANEL_BUFFERS,)),
             pltpu.SemaphoreType.DMA((PANEL_BUFFERS,)),
         ],
     )

time: 320 us -> 317 us (level)
  no operation moved by 1% of the time
where the time goes in v9:
time: 317 us; the launch traced here: 316 us
  waiting for transfers between devices  166 us (52%)
  blocking collectives  89.2 us (28%)
  Pallas kernels  30 us (9%)
  between operations  13.8 us (4%)
  matrix products  9.26 us (3%)
  local copies, waits for them, and re-layouts  4.49 us (1%)
  other arithmetic  3.73 us (1%)
    all_gather x1, waiting for transfers between devices, shards(): grad_panels = lax.all_gather(scaled_grad, 'rows', axis=0, tiled=True)  73 us
    reduce_scatter x1, waiting for transfers between devices, shards(): lax.psum_scatter(slab_part, 'rep', scatter_dimension=0, tiled=True)  45.9 us
    all_gather x1, waiting for transfers between devices, shards(): panels = lax.all_gather(scaled, 'rows', axis=0, tiled=True)  39.9 us
    all_to_all x2, blocking collectives, gather_by_exchange(): lax.all_to_all(copies, axis, 0, 0, tiled=True)  35.5 us
    pallas_call x2, Pallas kernels, aggregate_slots(): pl.pallas_call(_aggregate_kernel, grid_spec=grid_spec, out_shape=jax.Shap...  30 us
    all_to_all x1, blocking collectives, all_reduce_by_exchange(): lax.all_to_all(value.reshape(count, rows // count, width), axes, 0, 0, ti...  27.6 us
    all_to_all x1, blocking collectives, all_reduce_by_exchange(): return lax.all_to_all(spread, axes, 0, 0, tiled=True).reshape(rows, width)  26.1 us
    reduce_scatter x1, waiting for transfers between devices, shards(): lax.psum_scatter(back_part, 'rep', scatter_dimension=0, tiled=True)  7.01 us
  transfers between devices with their start and end apart: 4, of which 4 were waited for; matrix products, arithmetic and copies ran while one was open for 3% of the time, Pallas kernels for 0%

profile of v9, /device:TPU:1, one launch (start us, length us, event | category | flops | bytes accessed | tf_op | source)
XLA Modules:
  0.0 316.5 jit_solution(2727107430563318394)
XLA Ops:
  7.2 0.7 convert_rsqrt_fusion
  8.0 0.3 copy-done
  8.2 2.3 fusion.3
  10.5 0.0 reduce-scatter.3.cloned.1.call-start
  10.6 9.0 %all_to_all.20 = f32[4,512,1]{1,2,0:T(1,128)S(1)} all-to-all(f32[4,512,1]{1,2,0:T(1,128)S(1)} %broadcast_in_dim.7), channel_id=1, replica_groups=mesh['rows'=32,'rep'=4] {'rep'}, dimensions={0} | all-to-all | bytes 16384 | tf_op jit(solution)/shard_map/all_to_all | solution.py:91
  19.6 1.2 broadcast_in_dim.6
  20.8 26.5 %all_to_all.21 = bf16[4,512,512]{2,1,0:T(8,128)(2,1)S(1)} all-to-all(bf16[4,512,512]{2,1,0:T(8,128)(2,1)S(1)} %broadcast_in_dim.6), channel_id=1, replica_groups=mesh['rows'=32,'rep'=4] {'rep'}, dimensions={0} | all-to-all | bytes 4194304 | tf_op jit(solution)/shard_map/all_to_all | solution.py:91
  47.3 39.9 %all-gather.3.cloned.1.call-done.panels_hbm = bf16[16384,512]{1,0:T(8,128)(2,1)} async-done(((bf16[512,512]{1,0:T(8,128)(2,1)}), bf16[16384,512]{1,0:T(8,128)(2,1)}) %all-gather.3.cloned.1.call-update) | async-done | bytes 16777232 | tf_op jit(solution)/shard_map/all_gather | solution.py:103
  87.1 15.0 %shard_map.103 = f32[2048,512]{1,0:T(8,128)} custom-call(s32[64]{0:T(128)} %rows_ref.3, s32[64]{0:T(128)} %cols_ref.3, bf16[64,128,128]{2,1,0:T(8,128)(2,1)} %tiles_hbm.3, bf16[16384,512]{1,0:T(8,128)(2,1)} %all-gather.3.cloned.1.call-done.panels_hbm), custom_call_target="tpu_custom_call" | custom-call | tf_op jit(solution)/shard_map/pallas_call | solution.py:69
  102.2 0.0 all-gather.5.cloned.1.call-start
  102.3 45.9 %reduce-scatter.3.cloned.1.call-done = f32[512,512]{1,0:T(8,128)} async-done(((f32[2048,512]{1,0:T(8,128)}), f32[512,512]{1,0:T(8,128)}) %reduce-scatter.3.cloned.1.call-update) | async-done | bytes 1048592 | tf_op jit(solution)/shard_map/reduce_scatter | solution.py:108
  148.1 2.8 multiply_convert_fusion.1
  151.0 0.0 reduce-scatter.5.cloned.1.call-start
  151.0 73.0 %all-gather.5.cloned.1.call-done.panels_hbm = bf16[16384,512]{1,0:T(8,128)(2,1)} async-done(((bf16[512,512]{1,0:T(8,128)(2,1)}), bf16[16384,512]{1,0:T(8,128)(2,1)}) %all-gather.5.cloned.1.call-update) | async-done | bytes 16777232 | tf_op jit(solution)/shard_map/all_gather | solution.py:114
  224.0 15.0 %shard_map.104 = f32[2048,512]{1,0:T(8,128)} custom-call(s32[64]{0:T(128)} %rows_ref.3, s32[64]{0:T(128)} %cols_ref.3, bf16[64,128,128]{2,1,0:T(8,128)(2,1)} %tiles_hbm.3, bf16[16384,512]{1,0:T(8,128)(2,1)} %all-gather.5.cloned.1.call-done.panels_hbm), custom_call_target="tpu_custom_call" | custom-call | tf_op jit(solution)/shard_map/pallas_call | solution.py:69
  239.0 4.5 %fusion = f32[512,512]{1,0:T(8,128)} fusion(bf16[2048,512]{1,0:T(8,128)(2,1)S(1)} %bitcast.7, f32[2048,512]{1,0:T(8,128)} %shard_map.104, f32[2048]{0:T(1024)S(1)} %bitcast.8), kind=kOutput, calls=%fused_computation | convolution fusion | flops 1074790400 | bytes 7348224 | tf_op jit(solution)/shard_map/dot_general | solution.py:121
  243.5 1.5 reshape.27
  245.0 27.6 %all_to_all.22 = f32[128,4,512]{2,1,0:T(4,128)S(1)} all-to-all(f32[128,4,512]{2,1,0:T(4,128)S(1)} %reshape.27), channel_id=1, replica_groups=mesh['rows'=32,'rep'=4] {'rows','rep'}, dimensions={0} | all-to-all | bytes 2097152 | tf_op jit(solution)/shard_map/all_to_all | solution.py:82
  272.6 0.2 reduce_sum.9
  272.9 0.1 broadcast_in_dim.8
  273.0 26.1 %all_to_all.23 = f32[128,4,512]{2,1,0:T(4,128)S(1)} all-to-all(f32[128,4,512]{2,1,0:T(4,128)S(1)} %broadcast_in_dim.8), channel_id=1, replica_groups=mesh['rows'=32,'rep'=4] {'rows','rep'}, dimensions={0} | all-to-all | bytes 2097152 | tf_op jit(solution)/shard_map/all_to_all | solution.py:85
  299.1 1.3 reshape.28
  300.4 7.0 %reduce-scatter.5.cloned.1.call-done = f32[512,512]{1,0:T(8,128)} async-done(((f32[2048,512]{1,0:T(8,128)}), f32[512,512]{1,0:T(8,128)}) %reduce-scatter.5.cloned.1.call-update) | async-done | bytes 1048592 | tf_op jit(solution)/shard_map/reduce_scatter | solution.py:116
  307.4 2.5 convolution_convert_fusion
  (11 shorter events, 0.1 us)
Async XLA Ops:
  7.2 1.1 copy-start
  7.2 80.0 %all-gather.3.cloned.1.call-start = ((), (), s32[]{:S(2)}) async-start(), calls=%async_computation.6 | async-start | bytes 17301504 | tf_op jit(solution)/shard_map/all_gather | solution.py:103
  10.5 137.6 %reduce-scatter.3.cloned.1.call-start = ((), (), s32[]{:S(2)}) async-start(), calls=%async_computation.7 | async-start | bytes 5242880 | tf_op jit(solution)/shard_map/reduce_scatter | solution.py:108
  102.2 46.0 %copy-start.1 = (bf16[512,512]{1,0:T(8,128)(2,1)S(1)}, bf16[512,512]{1,0:T(8,128)(2,1)}, u32[]{:S(2)}) copy-start(bf16[512,512]{1,0:T(8,128)(2,1)} %param.15) | copy-start | bytes 1572868
  102.2 46.0 %copy-start.2 = (f32[512]{0:T(512)S(1)}, f32[512]{0:T(512)}, u32[]{:S(2)}) copy-start(f32[512]{0:T(512)} %param.10) | copy-start | bytes 6148
  102.2 121.8 %all-gather.5.cloned.1.call-start = ((), (), s32[]{:S(2)}) async-start(), calls=%async_computation.8 | async-start | bytes 17301504 | tf_op jit(solution)/shard_map/all_gather | solution.py:114
  151.0 156.5 %reduce-scatter.5.cloned.1.call-start = ((), (), s32[]{:S(2)}) async-start(), calls=%async_computation.9 | async-start | bytes 5242880 | tf_op jit(solution)/shard_map/reduce_scatter | solution.py:116
Sparse Core Ops, SparseCore 0:
  10.8 76.2 all-gather.2
  102.3 45.7 reduce-scatter.2
  151.1 72.8 all-gather.4
  239.1 68.2 reduce-scatter.4

commit v10 on v9

--- a/solution.py
+++ b/solution.py
@@ -45,7 +45,7 @@
 
         return carry
 
-    lax.fori_loop(0, slot_count, step, 0, unroll=2)
+    lax.fori_loop(0, slot_count, step, 0, unroll=8)
 
 
 def aggregate_slots(panels, group_rows, group_cols, tiles, out_blocks):

time: 317 us -> 317 us (level)
  no operation moved by 1% of the time
where the time goes in v10:
time: 317 us; the launch traced here: 316 us
  waiting for transfers between devices  166 us (52%)
  blocking collectives  89.2 us (28%)
  Pallas kernels  30 us (9%)
  between operations  13.8 us (4%)
  matrix products  9.26 us (3%)
  local copies, waits for them, and re-layouts  4.49 us (1%)
  other arithmetic  3.73 us (1%)
    all_gather x1, waiting for transfers between devices, shards(): grad_panels = lax.all_gather(scaled_grad, 'rows', axis=0, tiled=True)  73 us
    reduce_scatter x1, waiting for transfers between devices, shards(): lax.psum_scatter(slab_part, 'rep', scatter_dimension=0, tiled=True)  45.9 us
    all_gather x1, waiting for transfers between devices, shards(): panels = lax.all_gather(scaled, 'rows', axis=0, tiled=True)  39.9 us
    all_to_all x2, blocking collectives, gather_by_exchange(): lax.all_to_all(copies, axis, 0, 0, tiled=True)  35.5 us
    pallas_call x2, Pallas kernels, aggregate_slots(): pl.pallas_call(_aggregate_kernel, grid_spec=grid_spec, out_shape=jax.Shap...  30 us
    all_to_all x1, blocking collectives, all_reduce_by_exchange(): lax.all_to_all(value.reshape(count, rows // count, width), axes, 0, 0, ti...  27.6 us
    all_to_all x1, blocking collectives, all_reduce_by_exchange(): return lax.all_to_all(spread, axes, 0, 0, tiled=True).reshape(rows, width)  26.1 us
    reduce_scatter x1, waiting for transfers between devices, shards(): lax.psum_scatter(back_part, 'rep', scatter_dimension=0, tiled=True)  7.01 us
  transfers between devices with their start and end apart: 4, of which 4 were waited for; matrix products, arithmetic and copies ran while one was open for 3% of the time, Pallas kernels for 0%

profile of v10, /device:TPU:1, one launch (start us, length us, event | category | flops | bytes accessed | tf_op | source)
XLA Modules:
  0.0 316.5 jit_solution(8968590163924718428)
XLA Ops:
  7.2 0.7 convert_rsqrt_fusion
  8.0 0.3 copy-done
  8.2 2.3 fusion.3
  10.5 0.0 reduce-scatter.3.cloned.1.call-start
  10.6 9.0 %all_to_all.20 = f32[4,512,1]{1,2,0:T(1,128)S(1)} all-to-all(f32[4,512,1]{1,2,0:T(1,128)S(1)} %broadcast_in_dim.7), channel_id=1, replica_groups=mesh['rows'=32,'rep'=4] {'rep'}, dimensions={0} | all-to-all | bytes 16384 | tf_op jit(solution)/shard_map/all_to_all | solution.py:91
  19.6 1.2 broadcast_in_dim.6
  20.8 26.5 %all_to_all.21 = bf16[4,512,512]{2,1,0:T(8,128)(2,1)S(1)} all-to-all(bf16[4,512,512]{2,1,0:T(8,128)(2,1)S(1)} %broadcast_in_dim.6), channel_id=1, replica_groups=mesh['rows'=32,'rep'=4] {'rep'}, dimensions={0} | all-to-all | bytes 4194304 | tf_op jit(solution)/shard_map/all_to_all | solution.py:91
  47.3 39.9 %all-gather.3.cloned.1.call-done.panels_hbm = bf16[16384,512]{1,0:T(8,128)(2,1)} async-done(((bf16[512,512]{1,0:T(8,128)(2,1)}), bf16[16384,512]{1,0:T(8,128)(2,1)}) %all-gather.3.cloned.1.call-update) | async-done | bytes 16777232 | tf_op jit(solution)/shard_map/all_gather | solution.py:103
  87.1 15.0 %shard_map.103 = f32[2048,512]{1,0:T(8,128)} custom-call(s32[64]{0:T(128)} %rows_ref.3, s32[64]{0:T(128)} %cols_ref.3, bf16[64,128,128]{2,1,0:T(8,128)(2,1)} %tiles_hbm.3, bf16[16384,512]{1,0:T(8,128)(2,1)} %all-gather.3.cloned.1.call-done.panels_hbm), custom_call_target="tpu_custom_call" | custom-call | tf_op jit(solution)/shard_map/pallas_call | solution.py:69
  102.2 0.0 all-gather.5.cloned.1.call-start
  102.3 45.9 %reduce-scatter.3.cloned.1.call-done = f32[512,512]{1,0:T(8,128)} async-done(((f32[2048,512]{1,0:T(8,128)}), f32[512,512]{1,0:T(8,128)}) %reduce-scatter.3.cloned.1.call-update) | async-done | bytes 1048592 | tf_op jit(solution)/shard_map/reduce_scatter | solution.py:108
  148.1 2.8 multiply_convert_fusion.1
  151.0 0.0 reduce-scatter.5.cloned.1.call-start
  151.0 73.0 %all-gather.5.cloned.1.call-done.panels_hbm = bf16[16384,512]{1,0:T(8,128)(2,1)} async-done(((bf16[512,512]{1,0:T(8,128)(2,1)}), bf16[16384,512]{1,0:T(8,128)(2,1)}) %all-gather.5.cloned.1.call-update) | async-done | bytes 16777232 | tf_op jit(solution)/shard_map/all_gather | solution.py:114
  224.0 15.0 %shard_map.104 = f32[2048,512]{1,0:T(8,128)} custom-call(s32[64]{0:T(128)} %rows_ref.3, s32[64]{0:T(128)} %cols_ref.3, bf16[64,128,128]{2,1,0:T(8,128)(2,1)} %tiles_hbm.3, bf16[16384,512]{1,0:T(8,128)(2,1)} %all-gather.5.cloned.1.call-done.panels_hbm), custom_call_target="tpu_custom_call" | custom-call | tf_op jit(solution)/shard_map/pallas_call | solution.py:69
  239.0 4.5 %fusion = f32[512,512]{1,0:T(8,128)} fusion(bf16[2048,512]{1,0:T(8,128)(2,1)S(1)} %bitcast.7, f32[2048,512]{1,0:T(8,128)} %shard_map.104, f32[2048]{0:T(1024)S(1)} %bitcast.8), kind=kOutput, calls=%fused_computation | convolution fusion | flops 1074790400 | bytes 7348224 | tf_op jit(solution)/shard_map/dot_general | solution.py:121
  243.5 1.5 reshape.27
  245.0 27.6 %all_to_all.22 = f32[128,4,512]{2,1,0:T(4,128)S(1)} all-to-all(f32[128,4,512]{2,1,0:T(4,128)S(1)} %reshape.27), channel_id=1, replica_groups=mesh['rows'=32,'rep'=4] {'rows','rep'}, dimensions={0} | all-to-all | bytes 2097152 | tf_op jit(solution)/shard_map/all_to_all | solution.py:82
  272.6 0.2 reduce_sum.9
  272.9 0.1 broadcast_in_dim.8
  273.0 26.1 %all_to_all.23 = f32[128,4,512]{2,1,0:T(4,128)S(1)} all-to-all(f32[128,4,512]{2,1,0:T(4,128)S(1)} %broadcast_in_dim.8), channel_id=1, replica_groups=mesh['rows'=32,'rep'=4] {'rows','rep'}, dimensions={0} | all-to-all | bytes 2097152 | tf_op jit(solution)/shard_map/all_to_all | solution.py:85
  299.1 1.3 reshape.28
  300.4 7.0 %reduce-scatter.5.cloned.1.call-done = f32[512,512]{1,0:T(8,128)} async-done(((f32[2048,512]{1,0:T(8,128)}), f32[512,512]{1,0:T(8,128)}) %reduce-scatter.5.cloned.1.call-update) | async-done | bytes 1048592 | tf_op jit(solution)/shard_map/reduce_scatter | solution.py:116
  307.4 2.5 convolution_convert_fusion
  (11 shorter events, 0.1 us)
Async XLA Ops:
  7.2 1.1 copy-start
  7.2 80.0 %all-gather.3.cloned.1.call-start = ((), (), s32[]{:S(2)}) async-start(), calls=%async_computation.6 | async-start | bytes 17301504 | tf_op jit(solution)/shard_map/all_gather | solution.py:103
  10.5 137.6 %reduce-scatter.3.cloned.1.call-start = ((), (), s32[]{:S(2)}) async-start(), calls=%async_computation.7 | async-start | bytes 5242880 | tf_op jit(solution)/shard_map/reduce_scatter | solution.py:108
  102.2 46.0 %copy-start.1 = (bf16[512,512]{1,0:T(8,128)(2,1)S(1)}, bf16[512,512]{1,0:T(8,128)(2,1)}, u32[]{:S(2)}) copy-start(bf16[512,512]{1,0:T(8,128)(2,1)} %param.15) | copy-start | bytes 1572868
  102.2 46.0 %copy-start.2 = (f32[512]{0:T(512)S(1)}, f32[512]{0:T(512)}, u32[]{:S(2)}) copy-start(f32[512]{0:T(512)} %param.10) | copy-start | bytes 6148
  102.2 121.8 %all-gather.5.cloned.1.call-start = ((), (), s32[]{:S(2)}) async-start(), calls=%async_computation.8 | async-start | bytes 17301504 | tf_op jit(solution)/shard_map/all_gather | solution.py:114
  151.0 156.5 %reduce-scatter.5.cloned.1.call-start = ((), (), s32[]{:S(2)}) async-start(), calls=%async_computation.9 | async-start | bytes 5242880 | tf_op jit(solution)/shard_map/reduce_scatter | solution.py:116
Sparse Core Ops, SparseCore 0:
  10.8 76.2 all-gather.2
  102.3 45.7 reduce-scatter.2
  151.1 72.8 all-gather.4
  239.1 68.2 reduce-scatter.4
